TPU v7x, 32 devices: a whole 2x2x4 slice. The times are simulated.
32 devices in a mesh: groups: 2 (over y), ctx: 4 (over z), chan: 4 (over x, core).
Axes of the slice: x: 2, y: 2, z: 4, core: 2. Of those that a mesh axis runs over, the one named last changes fastest.
Arguments:
- q_feat: bfloat16 [4096, 8192], P(('groups', 'ctx'), 'chan'), parts along dimension 0, may hold values from -6 to 6
- k_feat: bfloat16 [4096, 8192], P(('groups', 'ctx'), 'chan'), parts along dimension 0, may hold values from -6 to 6
- v_feat: bfloat16 [4096, 8192], P(('groups', 'ctx'), 'chan'), parts along dimension 0, may hold values from -6 to 6
- pole_rate: float32 [16, 8192], P(None, 'chan'), may hold values from 4.8828126e-05 to 0.03
- residue: float32 [16, 8192], P(None, 'chan'), may hold values from -1.5 to 1.5
- skip_gain: float32 [8192], P('chan'), may hold values from 0.5 to 1.5
- lengths: int32 [8], P('groups'), parts along dimension 0, may hold values from 1 to 1024, 2048 in all
- owners: int32 [8], P('groups'), parts along dimension 0, may hold values from 0 to 3, as said below
Outputs:
- mixed_out: bfloat16 [4096, 8192], P(('groups', 'ctx'), 'chan'), parts along dimension 0
- decode_state: float32 [8, 16, 8192], P(('groups', 'ctx'), None, 'chan'), parts along dimension 0
There are 2 independent parts, one for each index of `groups`. A program takes and returns all parts, laid end to end along the dimension named above; an argument that names none is the same for every part. Nothing has to cross between parts.
Inputs may be any that keep to these rules, and one draw needn't show every extreme that they name: The 4 lengths sum to 2048; the longest is exactly 1024. The 4 owners are distinct.
All inputs are finite; a program needn't handle non-finite values.
Results may differ from a plain program's by a relative error of at most 0.001.
Values sent between devices are 32-bit elements; how exact they have to be, the bound alone decides.
A program may use at most 128 MiB of HBM per device.

v0:
```python
import functools

import jax
import jax.numpy as jnp
from jax import lax
from jax.experimental import pallas as pl
from jax.experimental.pallas import tpu as pltpu
from jax.sharding import PartitionSpec as P

F32 = jnp.float32
LANES = 128
ROWS = 8
UNROLL = 8
DEEP = 16


def spans(lens_ref, count, tok):
    first = lax.axis_index("ctx") * tok
    offset = jnp.int32(0)
    found = []
    for r in range(count):
        size = lens_ref[r]
        end = offset + size
        lo = jnp.clip(offset - first, 0, tok)
        hi = jnp.clip(end - first, 0, tok)
        found.append((lo, hi, offset < first, end > first, end <= first + tok, end - first))
        offset = end
    return found


def spread(value, dst_ref, sub, base=0):
    for i in range(value.shape[0] // ROWS):
        for j in range(sub):
            dst_ref[pl.ds(base + i * ROWS * sub + j, ROWS, stride=sub), :] = value[
                i * ROWS : (i + 1) * ROWS, j * LANES : (j + 1) * LANES
            ]


def unspread(src_ref, dst_ref, count, sub):
    for i in range(count // ROWS):
        for j in range(sub):
            dst_ref[i * ROWS : (i + 1) * ROWS, j * LANES : (j + 1) * LANES] = src_ref[
                pl.ds(i * ROWS * sub + j, ROWS, stride=sub), :
            ]


def walk(lo, hi, step, state):
    groups = (hi - lo) // UNROLL

    def many(i, state):
        start = lo + i * UNROLL
        for k in range(UNROLL):
            state = step(start + k, state)
        return state

    state = lax.fori_loop(0, groups, many, state)
    return lax.fori_loop(lo + groups * UNROLL, hi, step, state)


def ends_kernel(
    lens_ref, own_ref, k_ref, v_ref, rate_ref, u_ref, end_ref, span_ref, base_ref, coef_ref,
    decay_sc, state_sc, *, tok, sub, poles, count, chunk,
):
    rate = rate_ref[...]
    spread(jnp.exp(-rate), decay_sc, sub)

    def mix(i, _):
        start = pl.multiple_of(i * chunk, chunk)
        u = k_ref[pl.ds(start, chunk), :].astype(F32) * v_ref[pl.ds(start, chunk), :].astype(F32)
        spread(u, u_ref, sub, start * sub)
        return 0

    lax.fori_loop(0, tok // chunk, mix, 0)
    decay = [decay_sc[p * sub : (p + 1) * sub, :] for p in range(poles)]

    def step(t, state):
        u = u_ref[pl.ds(pl.multiple_of(t * sub, sub), sub), :]
        return tuple(d * s + u for d, s in zip(decay, state))

    base_ref[...] = jnp.zeros_like(base_ref)
    coef_ref[...] = jnp.zeros_like(coef_ref)
    span_ref[...] = jnp.zeros_like(span_ref)
    zero = tuple(jnp.zeros((sub, LANES), F32) for _ in range(poles))
    for r, (lo, hi, before, reaches, ends, steps) in enumerate(spans(lens_ref, count, tok)):

        @pl.when(hi > lo)
        def _():
            state = walk(lo, hi, step, zero)
            for p in range(poles):
                state_sc[p * sub : (p + 1) * sub, :] = state[p]

            @pl.when(hi == tok)
            def _():
                unspread(state_sc, end_ref, poles, sub)

            @pl.when(ends)
            def _():
                unspread(state_sc, base_ref.at[own_ref[r]], poles, sub)

            @pl.when(before & ends)
            def _():
                coef_ref[own_ref[r]] = jnp.exp(rate * -steps.astype(F32))

            @pl.when(before & (hi == tok))
            def _():
                span_ref[...] = jnp.exp(rate * -float(tok))


def conv_kernel(
    lens_ref, end_ref, span_ref, base_ref, coef_ref, rate_ref, res_ref, gain_ref, u_hbm, q_hbm,
    out_hbm, got_ref,
    arrived, passed, slotted, landed, decay_sc, res_sc, state_sc, gain_sc, conv_sc,
    u_ref, q_ref, out_ref, sent_sem, come_sem, give_sem, take_sem, load_sem, store_sem,
    *, hops, parts, tok, sub, poles, count, chunk, tiles,
):
    slots, _, channels = base_ref.shape
    width = channels // parts
    wide = sub * LANES
    rows_in = tok * sub
    me = lax.axis_index("ctx")
    barrier = pltpu.get_barrier_semaphore()
    peers = [lax.rem(me + j, slots) for j in range(1, slots)]
    for peer in peers:
        pl.semaphore_signal(
            barrier, inc=1, device_id={"ctx": peer}, device_id_type=pl.DeviceIdType.MESH
        )
    loads = []
    for i in range(tiles):
        flat, cols = pl.ds(i * rows_in, rows_in), pl.ds(i * wide, wide)
        loads.append(
            (
                pltpu.make_async_copy(u_hbm.at[flat, :], u_ref.at[flat, :], load_sem.at[i, 0]),
                pltpu.make_async_copy(q_hbm.at[:, cols], q_ref.at[:, cols], load_sem.at[i, 1]),
            )
        )
        loads[i][0].start()
        loads[i][1].start()
    pl.semaphore_wait(barrier, slots - 1)

    def lanes(part):
        return pl.ds(part * width, width)

    def pass_on(hop, part):
        source = end_ref if hop == 0 else passed.at[hop - 1]
        return pltpu.make_async_remote_copy(
            src_ref=source.at[:, lanes(part)],
            dst_ref=arrived.at[hop, :, lanes(part)],
            send_sem=sent_sem.at[hop, part],
            recv_sem=come_sem.at[hop, part],
            device_id={"ctx": lax.rem(me + 1, slots)},
            device_id_type=pl.DeviceIdType.MESH,
        )

    def give(j, part):
        return pltpu.make_async_remote_copy(
            src_ref=slotted.at[j - 1, :, lanes(part)],
            dst_ref=landed.at[j - 1, :, lanes(part)],
            send_sem=give_sem.at[j - 1, part],
            recv_sem=take_sem.at[j - 1, part],
            device_id={"ctx": peers[j - 1]},
            device_id_type=pl.DeviceIdType.MESH,
        )

    def arrive(hop, part):
        @pl.when(me > 0)
        def _():
            pass_on(hop, part).wait_recv()

    def hop_on(hop, part):
        if hop:
            arrive(hop - 1, part)
            at = lanes(part)
            passed[hop - 1, :, at] = span_ref[:, at] * arrived[hop - 1, :, at] + end_ref[:, at]

        @pl.when(me < slots - 1)
        def _():
            pass_on(hop, part).start()

    def finish(part):
        arrive(hops - 1, part)
        at = lanes(part)
        incoming = arrived[hops - 1, :, at]
        for j in range(1, slots):
            slotted[j - 1, :, at] = (
                base_ref[peers[j - 1], :, at] + coef_ref[peers[j - 1], :, at] * incoming
            )
            give(j, part).start()
        got_ref[0, :, at] = base_ref[me, :, at] + coef_ref[me, :, at] * incoming

    @pl.when(me == 0)
    def _():
        arrived[...] = jnp.zeros_like(arrived)

    for hop in range(hops):
        for part in range(parts):
            hop_on(hop, part)

    first = me * tok
    offset = jnp.int32(0)
    starts = []
    for r in range(count):
        starts.append(offset - first)
        offset = offset + lens_ref[r]

    def conv(i, begin, stop):
        scale = [res_sc[p] for p in range(poles)]
        gain = gain_sc[...]

        def many(n, state):
            for k in range(DEEP):
                t = n * DEEP + k
                keep = jnp.int32(1)
                for at in starts:
                    keep = keep - (t == at).astype(jnp.int32)
                pick = jnp.maximum(keep, 0) * poles
                rows = pl.ds(pl.multiple_of(t * sub, sub), sub)
                u = u_ref[pl.ds(pl.multiple_of(i * rows_in + t * sub, sub), sub), :]
                state = tuple(decay_sc[pick + p] * s + u for p, s in enumerate(state))
                terms = [gain * u] + [c * s for c, s in zip(scale, state)]
                while len(terms) > 1:
                    terms = [a + b for a, b in zip(terms[::2], terms[1::2])] + (
                        [terms[-1]] if len(terms) % 2 else []
                    )
                conv_sc[rows, :] = terms[0]
            return state

        state = tuple(state_sc[p] for p in range(poles))
        state = lax.fori_loop(begin // DEEP, stop // DEEP, many, state)
        for p in range(poles):
            state_sc[p] = state[p]

    def scatter(value, ref, base):
        for p in range(poles):
            for j in range(sub):
                ref[base + p, j : j + 1, :] = value[p : p + 1, j * LANES : (j + 1) * LANES]

    stores = []
    per_tile = parts // tiles
    for i in range(tiles):
        cols = slice(i * wide, (i + 1) * wide)
        rate = rate_ref[:, cols]
        decay_sc[0:poles] = jnp.zeros((poles, sub, LANES), F32)
        scatter(jnp.exp(-rate), decay_sc, poles)
        scatter(res_ref[:, cols] * jnp.sqrt(1.0 - jnp.exp(-2.0 * rate)), res_sc, 0)
        for j in range(sub):
            at = i * wide + j * LANES
            gain_sc[j : j + 1, :] = gain_ref[0:1, at : at + LANES]
        if i == 0:
            for part in range(per_tile):
                finish(part)
        scatter(arrived[hops - 1, :, cols], state_sc, 0)
        loads[i][0].wait()
        if i == 0 and tiles > 1:
            conv(i, 0, tok // 4)
            for part in range(per_tile, parts):
                finish(part)
            conv(i, tok // 4, tok)
        else:
            conv(i, 0, tok)
        loads[i][1].wait()

        def gate(n, _):
            start = pl.multiple_of(n * chunk, chunk)
            rows = pl.ds(start, chunk)
            for j in range(sub):
                at = slice(i * wide + j * LANES, i * wide + (j + 1) * LANES)
                value = conv_sc[pl.ds(start * sub + j, chunk, stride=sub), :]
                out_ref[rows, at] = (q_ref[rows, at].astype(F32) * value).astype(out_ref.dtype)
            return 0

        lax.fori_loop(0, tok // chunk, gate, 0)
        stores.append(
            pltpu.make_async_copy(
                out_ref.at[:, pl.ds(i * wide, wide)], out_hbm.at[:, pl.ds(i * wide, wide)],
                store_sem.at[i],
            )
        )
        stores[i].start()

    for part in range(parts):
        at = lanes(part)
        for j in range(1, slots):
            give(j, part).wait_recv()
        total = got_ref[0, :, at]
        for j in range(1, slots):
            total += landed[j - 1, :, at]
        got_ref[0, :, at] = total
    for part in range(parts):
        for j in range(1, slots):
            give(j, part).wait_send()

    @pl.when(me < slots - 1)
    def _():
        for hop in range(hops):
            for part in range(parts):
                pass_on(hop, part).wait_send()

    for copy in stores:
        copy.wait()


def shards(q_feat, k_feat, v_feat, pole_rate, residue, skip_gain, lengths, owners):
    tok, channels = q_feat.shape
    poles, count = pole_rate.shape[0], lengths.shape[0]
    slots = lax.axis_size("ctx")
    sub = min(ROWS, channels // LANES)
    width = sub * LANES
    tiles = channels // width
    sizes = dict(tok=tok, sub=sub, poles=poles, count=count, chunk=16)
    feat = pl.BlockSpec((tok, width), lambda i, *_: (0, i))
    pole = pl.BlockSpec((poles, width), lambda i, *_: (0, i))
    slot = pl.BlockSpec((slots, poles, width), lambda i, *_: (0, 0, i))
    flat = pl.BlockSpec((tok * sub, LANES), lambda i, *_: (i, 0))
    small = pltpu.VMEM((poles * sub, LANES), F32)
    elems = tok * channels
    mixed, end, span, base, coef = pl.pallas_call(
        functools.partial(ends_kernel, **sizes),
        grid_spec=pltpu.PrefetchScalarGridSpec(
            num_scalar_prefetch=2,
            grid=(tiles,),
            in_specs=[feat, feat, pole],
            out_specs=[flat, pole, pole, slot, slot],
            scratch_shapes=[small, small],
        ),
        out_shape=[
            jax.ShapeDtypeStruct((tiles * tok * sub, LANES), F32),
            jax.ShapeDtypeStruct((poles, channels), F32),
            jax.ShapeDtypeStruct((poles, channels), F32),
            jax.ShapeDtypeStruct((slots, poles, channels), F32),
            jax.ShapeDtypeStruct((slots, poles, channels), F32),
        ],
        cost_estimate=pl.CostEstimate(
            flops=2 * poles * elems, bytes_accessed=8 * elems, transcendentals=0
        ),
        name="ends",
    )(lengths, owners, k_feat, v_feat, pole_rate)

    longest = tok * slots // 2
    hops = min((longest - 2) // tok + 1, slots - 1)
    parts = max(tiles, min(4, channels // LANES))
    dma = pltpu.SemaphoreType.DMA
    vmem, hbm = pl.BlockSpec(memory_space=pltpu.VMEM), pl.BlockSpec(memory_space=pl.ANY)
    mixed_out, decode_state = pl.pallas_call(
        functools.partial(conv_kernel, hops=hops, parts=parts, tiles=tiles, **sizes),
        in_specs=[pl.BlockSpec(memory_space=pltpu.SMEM)] + [vmem] * 7 + [hbm] * 2,
        out_specs=[hbm, vmem],
        out_shape=[
            jax.ShapeDtypeStruct((tok, channels), q_feat.dtype),
            jax.ShapeDtypeStruct((1, poles, channels), F32),
        ],
        scratch_shapes=[
            pltpu.VMEM((hops, poles, channels), F32),
            pltpu.VMEM((max(hops - 1, 1), poles, channels), F32),
            pltpu.VMEM((slots - 1, poles, channels), F32),
            pltpu.VMEM((slots - 1, poles, channels), F32),
            pltpu.VMEM((2 * poles, sub, LANES), F32),
            pltpu.VMEM((poles, sub, LANES), F32),
            pltpu.VMEM((poles, sub, LANES), F32),
            pltpu.VMEM((sub, LANES), F32),
            pltpu.VMEM((tok * sub, LANES), F32),
            pltpu.VMEM((tiles * tok * sub, LANES), F32),
            pltpu.VMEM((tok, channels), q_feat.dtype),
            pltpu.VMEM((tok, channels), q_feat.dtype),
            dma((hops, parts)), dma((hops, parts)),
            dma((slots - 1, parts)), dma((slots - 1, parts)),
            dma((tiles, 2)), dma((tiles,)),
        ],
        compiler_params=pltpu.CompilerParams(collective_id=0, has_side_effects=True),
        name="conv",
    )(
        lengths, end, span, base, coef, pole_rate, residue, skip_gain[None, :], mixed, q_feat
    )
    return mixed_out, decode_state


def solution(mesh):
    tokens = P(("groups", "ctx"), "chan")
    return jax.shard_map(
        shards,
        mesh=mesh,
        in_specs=(
            tokens, tokens, tokens, P(None, "chan"), P(None, "chan"), P("chan"),
            P("groups"), P("groups"),
        ),
        out_specs=(tokens, P(("groups", "ctx"), None, "chan")),
        check_vma=False,
    )
```

profile of v0, /device:TPU:0, one launch (start us, length us, event | category | flops | bytes accessed | tf_op | source)
XLA Modules:
  0.0 39.5 jit_solution(16844573038139662240)
XLA Ops:
  0.6 10.1 %ends.1 = (f32[8192,128]{1,0:T(8,128)}, f32[16,2048]{1,0:T(8,128)}, f32[16,2048]{1,0:T(8,128)}, f32[4,16,2048]{2,1,0:T(8,128)}, f32[4,16,2048]{2,1,0:T(8,128)}) custom-call(s32[4]{0:T(128)} %lens_ref.3, s32[4]{0:T(128)} %own_ref.1, bf16[512,2048]{1,0:T(8,128)(2,1)} %k_ref.1, bf16[512,2048]{1,0:T(8,128)(2,1)} %v_ref.1, f32[16,2048]{1,0:T(8,128)} %rate_ref.3), custom_call_target="tpu_custom_call" | custom-call | flops 33554432 | bytes 8388608 | tf_op jit(solution)/shard_map/ends/pallas_call | solution.py:316
  10.7 24.9 %conv.1 = (bf16[512,2048]{1,0:T(8,128)(2,1)}, f32[1,16,2048]{2,1,0:T(8,128)}) custom-call(s32[4]{0:T(128)} %lens_ref.3, f32[16,2048]{1,0:T(8,128)} %get-tuple-element.7.end_ref, f32[16,2048]{1,0:T(8,128)} %get-tuple-element.8.span_ref, f32[4,16,2048]{2,1,0:T(8,128)} %get-tuple-element.9.base_ref, f32[4,16,2048]{2,1,0:T(8,128)} %get-tuple-element.10.coef_ref, ...), custom_call_target="tpu_custom_call" | custom-call | tf_op jit(solution)/shard_map/conv/pallas_call | solution.py:343
  35.6 0.0 copy-start
  35.6 3.2 %copy.12 = bf16[512,2048]{1,0:T(8,128)(2,1)} copy(bf16[512,2048]{1,0:T(8,128)(2,1)} %get-tuple-element.14) | data formatting | bytes 4194304
  38.8 0.0 copy-done
  38.8 0.7 %copy.13 = f32[1,16,2048]{2,1,0:T(8,128)} copy(f32[1,16,2048]{2,1,0:T(8,128)S(1)} %copy-done) | data formatting | bytes 262144
Async XLA Ops:
  35.6 3.2 %copy-start = (f32[1,16,2048]{2,1,0:T(8,128)S(1)}, f32[1,16,2048]{2,1,0:T(8,128)}, u32[]{:S(2)}) copy-start(f32[1,16,2048]{2,1,0:T(8,128)} %get-tuple-element.15) | copy-start | bytes 393220
where the time goes:
time: 39.9 us; the launch traced here: 39.5 us
  Pallas kernels  35 us (88%)
  local copies, waits for them, and re-layouts  3.85 us (10%)
  between operations  0.65 us (2%)
    pallas_call x1, Pallas kernels, shards(): pl.pallas_call(functools.partial(conv_kernel, hops=hops, parts=parts, til...  24.9 us
    pallas_call x1, Pallas kernels, shards(): pl.pallas_call(functools.partial(ends_kernel, **sizes), grid_spec=pltpu.P...  10.1 us
    unnamed x4, local copies, waits for them, and re-layouts  3.85 us

commit v1 on v0

v1 whole, which is shorter than its diff:
```python
import functools

import jax
import jax.numpy as jnp
from jax import lax
from jax.experimental import pallas as pl
from jax.experimental.pallas import tpu as pltpu
from jax.sharding import PartitionSpec as P

F32 = jnp.float32
LANES = 128
ROWS = 8
MESH = pl.DeviceIdType.MESH


def lane(c):
    if isinstance(c, int):
        return pl.ds(c * LANES, LANES)
    return pl.ds(pl.multiple_of(c * LANES, LANES), LANES)


def kernel(
    lens_ref, own_ref, rate_hbm, res_hbm, gain_hbm, k_hbm, v_hbm, q_hbm,
    out_ref, dec_ref,
    k_ref, v_ref, q_ref, rate_ref, res_ref, gain_ref, u_ref, um_ref, s_ref, w_ref,
    dtab, etab, ftab, cs_ref, mtab, fix_ref, tbuf,
    arrived, passed, arr_r, put_r, arr_l, put_l,
    where_ref, kind_ref, inside_ref, par_sem, kv_sem, q_sem, st_send, st_recv, r_send, r_recv, l_send, l_recv,
    *, tok, poles, count, cols, per,
):
    slots = lax.axis_size("ctx")
    last = slots - 1
    me = lax.axis_index("ctx")
    tiles = cols // per
    halves = poles // ROWS
    chunks = tok // ROWS
    width = per * LANES
    barrier = pltpu.get_barrier_semaphore()

    @pl.when(me > 0)
    def _():
        pl.semaphore_signal(barrier, inc=1, device_id={"ctx": me - 1}, device_id_type=MESH)

    @pl.when(me < last)
    def _():
        pl.semaphore_signal(barrier, inc=1, device_id={"ctx": me + 1}, device_id_type=MESH)

    params = [
        pltpu.make_async_copy(src, dst, par_sem.at[i])
        for i, (src, dst) in enumerate(
            [(rate_hbm, rate_ref), (res_hbm, res_ref), (gain_hbm, gain_ref)]
        )
    ]
    params[0].start()
    loads = []
    for t in range(tiles):
        at = pl.ds(t * width, width)
        loads.append(
            [
                pltpu.make_async_copy(src.at[:, at], dst.at[:, at], kv_sem.at[t, i])
                for i, (src, dst) in enumerate([(k_hbm, k_ref), (v_hbm, v_ref)])
            ]
        )
        for copy in loads[t]:
            copy.start()
    params[1].start()
    params[2].start()
    q_load = pltpu.make_async_copy(q_hbm, q_ref, q_sem)
    q_load.start()

    first = me * tok
    offset = jnp.int32(0)
    begin, final = [], []
    for r in range(count):
        begin.append(offset - first)
        offset = offset + lens_ref[r]
        final.append(offset - 1 - first)
    starts = begin[1:]
    inner = len(starts)
    zero_row = count + 1

    where_in = [lax.shift_right_arithmetic(a, 3) for a in starts]
    rel_in = [lax.bitwise_and(a, ROWS - 1) for a in starts]

    def last_in(n):
        found = jnp.int32(-1)
        for chunk, rel in zip(where_in, rel_in):
            found = jnp.maximum(found, jnp.where(chunk == n, rel, -1))
        return found

    def first_in(n):
        found = jnp.int32(ROWS)
        for chunk, rel in zip(where_in, rel_in):
            found = jnp.minimum(found, jnp.where(chunk == n, rel, ROWS))
        return found

    def keeps(n):
        hit = jnp.int32(1)
        for chunk in where_in:
            hit = jnp.where(chunk == n, 0, hit)
        return hit

    covers = jnp.int32(1)
    ends_here, goes_on = [], []
    dist = jnp.int32(0)
    for a in starts:
        covers = jnp.where((a >= 0) & (a < tok), 0, covers)
    for r in range(count):
        ends_here.append((final[r] >= 0) & (final[r] < tok))
        goes_on.append((begin[r] < tok) & (final[r] >= tok))
        dist = jnp.where(goes_on[r], final[r] - (tok - 1), dist)

    def source_of(slot):
        row = jnp.int32(zero_row)
        for r in range(count):
            kind = jnp.where(ends_here[r], r, jnp.where(goes_on[r], count, zero_row))
            row = jnp.where(own_ref[r] == slot, kind, row)
        return row

    iota = lax.broadcasted_iota(jnp.int32, (ROWS, LANES), 0)

    def bcast(row):
        return jnp.broadcast_to(row, (ROWS, LANES))

    for n in range(ROWS + 1):
        mtab[n] = (iota < n).astype(F32)
    fix_ref[inner] = jnp.zeros((ROWS, LANES), F32)
    tbuf[zero_row] = jnp.zeros(tbuf.shape[1:], F32)
    dtab[0] = jnp.zeros(dtab.shape[1:], F32)
    dtab[2] = jnp.ones(dtab.shape[1:], F32)
    etab[0] = jnp.zeros(etab.shape[1:], F32)
    ftab[0] = jnp.zeros(ftab.shape[1:], F32)
    params[0].wait()
    rate = rate_ref[...]
    dtab[1] = jnp.exp(-rate)
    etab[1] = jnp.exp(rate * -float(ROWS))
    ftab[1] = jnp.exp(rate * -float(tok))
    ftab[2] = jnp.exp(rate * -dist.astype(F32))

    def part(h):
        return pl.ds(h * ROWS, ROWS)

    def mix(t):
        def body(m, _):
            for half in range(2):
                n = 4 * m + 2 * half
                rows = pl.ds(pl.multiple_of(n * ROWS, 2 * ROWS), 2 * ROWS)
                masks = [iota >= last_in(n + i) for i in range(2)]
                for c in range(t * per, (t + 1) * per):
                    u = k_ref[rows, lane(c)].astype(F32) * v_ref[rows, lane(c)].astype(F32)
                    u_ref[c, rows, :] = u
                    for i in range(2):
                        at = pl.ds(pl.multiple_of((n + i) * ROWS, ROWS), ROWS)
                        um_ref[c, at, :] = jnp.where(
                            masks[i], u[i * ROWS : (i + 1) * ROWS], 0.0
                        )
            return 0

        lax.fori_loop(0, chunks // 4, body, 0)

    def scan(t):
        pairs = [(c, h) for c in range(t * per, (t + 1) * per) for h in range(halves)]

        def body(m, state):
            state = list(state)
            for i in range(4):
                n = 4 * m + i
                base = n * ROWS
                keep = keeps(n)
                for x, (c, h) in enumerate(pairs):
                    s_ref[c, n, part(h), :] = state[x]
                local = [None] * len(pairs)
                for j in range(ROWS):
                    rows = {
                        c: bcast(um_ref[c, pl.ds(base + j, 1), :])
                        for c in range(t * per, (t + 1) * per)
                    }
                    for x, (c, h) in enumerate(pairs):
                        if j == 0:
                            local[x] = rows[c]
                        else:
                            local[x] = dtab[1, part(h), lane(c)] * local[x] + rows[c]
                for x, (c, h) in enumerate(pairs):
                    state[x] = etab[keep, part(h), lane(c)] * state[x] + local[x]
            return tuple(state)

        zero = jnp.zeros((ROWS, LANES), F32)
        state = lax.fori_loop(0, chunks // 4, body, tuple(zero for _ in pairs))
        for x, (c, h) in enumerate(pairs):
            s_ref[c, chunks, part(h), :] = state[x]
            tbuf[count, part(h), lane(c)] = state[x] * ftab[2, part(h), lane(c)]

            @pl.when(me == 0)
            def _():
                passed[part(h), lane(c)] = state[x]

    for r in range(count):
        end = jnp.clip(final[r], 0, tok - 1)
        n = lax.shift_right_logical(end, 3)
        stop = end - n * ROWS
        b = begin[r] - n * ROWS
        where_ref[r] = n
        for j in range(ROWS):
            kind = jnp.where(j > stop, 2, jnp.where(j <= b, 0, 1))
            kind_ref[r, j] = jnp.where(ends_here[r], kind, 0)
            inside = ends_here[r] & (j >= b) & (j <= stop)
            inside_ref[r, j] = jnp.where(inside, 1.0, 0.0).astype(F32)

    def tails(t):
        for r in range(count):
            n = where_ref[r]
            kinds = [kind_ref[r, j] for j in range(ROWS)]
            weights = [inside_ref[r, j] for j in range(ROWS)]
            for c in range(t * per, (t + 1) * per):
                value = [s_ref[c, n, part(h), :] for h in range(halves)]
                for j in range(ROWS):
                    row = bcast(u_ref[c, pl.ds(n * ROWS + j, 1), :]) * weights[j]
                    value = [
                        dtab[kinds[j], part(h), lane(c)] * x + row for h, x in enumerate(value)
                    ]
                for h in range(halves):
                    tbuf[r, part(h), lane(c)] = value[h]

    def span(t):
        return pl.ds(t * width, width)

    def pass_on(t):
        return pltpu.make_async_remote_copy(
            src_ref=passed.at[:, span(t)], dst_ref=arrived.at[:, span(t)],
            send_sem=st_send.at[t], recv_sem=st_recv.at[t],
            device_id={"ctx": me + 1}, device_id_type=MESH,
        )

    def arrival(t):
        return pltpu.make_async_remote_copy(
            src_ref=passed.at[:, span(t)], dst_ref=arrived.at[:, span(t)],
            send_sem=st_send.at[t], recv_sem=st_recv.at[t],
            device_id={"ctx": me - 1}, device_id_type=MESH,
        )

    def relay(t):
        arrival(t).wait_recv()

        @pl.when(me < last)
        def _():
            for c in range(t * per, (t + 1) * per):
                for h in range(halves):
                    passed[part(h), lane(c)] = (
                        s_ref[c, chunks, part(h), :]
                        + ftab[covers, part(h), lane(c)] * arrived[part(h), lane(c)]
                    )
            pass_on(t).start()

    def to_right(i, t):
        return pltpu.make_async_remote_copy(
            src_ref=put_r.at[i, :, span(t)], dst_ref=arr_r.at[i, :, span(t)],
            send_sem=r_send.at[i, t], recv_sem=r_recv.at[i, t],
            device_id={"ctx": me + 1}, device_id_type=MESH,
        )

    def to_left(i, t):
        return pltpu.make_async_remote_copy(
            src_ref=put_l.at[i, :, span(t)], dst_ref=arr_l.at[i, :, span(t)],
            send_sem=l_send.at[i, t], recv_sem=l_recv.at[i, t],
            device_id={"ctx": me - 1}, device_id_type=MESH,
        )

    back = last - me

    def hop(i, t):
        at = span(t)

        @pl.when((me <= i) & (me < last))
        def _():
            own = tbuf[source_of(me + last - i), :, at]
            put_r[i, :, at] = own
            if i:

                @pl.when(me > 0)
                def _():
                    to_right(i - 1, t).wait_recv()
                    put_r[i, :, at] = own + arr_r[i - 1, :, at]

            to_right(i, t).start()

        @pl.when((back <= i) & (back < last))
        def _():
            own = tbuf[source_of(i - back), :, at]
            put_l[i, :, at] = own
            if i:

                @pl.when(back > 0)
                def _():
                    to_left(i - 1, t).wait_recv()
                    put_l[i, :, at] = own + arr_l[i - 1, :, at]

            to_left(i, t).start()

    hops = last
    points = 2 * tiles
    lag = 2

    def serve(point):
        for t in range(tiles):
            if point < points:
                due = (me > 0) & (t + lag * me == point)
            elif t == point - points:
                due = (me > 0) & (t + lag * me >= points)
            else:
                continue

            @pl.when(due)
            def _():
                relay(t)

    def taps(c):
        at = lane(c)
        steps = (iota + 1).astype(F32)
        total = jnp.zeros((ROWS, LANES), F32)
        head = bcast(gain_ref[0:1, at])
        for p in range(poles):
            scale = bcast(cs_ref[pl.ds(p, 1), at])
            value = scale * jnp.exp(bcast(rate_ref[pl.ds(p, 1), at]) * -steps)
            w_ref[c, p] = value
            total = total + value
            head = head + scale
        lead = jnp.where(iota == 0, head, pltpu.roll(total, 1, 0))
        taps = [lead] + [
            jnp.where(iota >= j, pltpu.roll(lead, j, 0), 0.0) for j in range(1, ROWS)
        ]
        for x, a in enumerate(starts):
            base = lax.shift_right_logical(jnp.clip(a, 0, tok - 1), 3) * ROWS
            value = jnp.zeros((ROWS, LANES), F32)
            for j in range(ROWS - 1):
                cut = jnp.int32(ROWS)
                for other in starts:
                    rel = other - base
                    cut = jnp.minimum(cut, jnp.where(rel > j, rel, ROWS))
                row = bcast(u_ref[c, pl.ds(base + j, 1), :])
                value = value - jnp.where(iota >= cut, taps[j], 0.0) * row
            fix_ref[x] = value

        def body(m, _):
            for i in range(4):
                n = m * 4 + i
                which = jnp.int32(inner)
                for x, chunk in enumerate(where_in):
                    which = jnp.where(chunk == n, x, which)
                acc = [fix_ref[which], None]
                for j in range(ROWS):
                    term = taps[j] * bcast(u_ref[c, pl.ds(n * ROWS + j, 1), :])
                    acc[j % 2] = term if acc[j % 2] is None else acc[j % 2] + term
                um_ref[c, pl.ds(pl.multiple_of(n * ROWS, ROWS), ROWS), :] = acc[0] + acc[1]
            return 0

        lax.fori_loop(0, chunks // 4, body, 0)

    def carry(t):
        pairs = [(c, h) for c in range(t * per, (t + 1) * per) for h in range(halves)]

        def body(m, state):
            state = list(state)
            for i in range(4):
                n = m * 4 + i
                keep = keeps(n)
                for x, (c, h) in enumerate(pairs):
                    s_ref[c, n, part(h), :] = s_ref[c, n, part(h), :] + state[x]
                    state[x] = etab[keep, part(h), lane(c)] * state[x]
            return tuple(state)

        lax.fori_loop(
            0, chunks // 4, body, tuple(arrived[part(h), lane(c)] for c, h in pairs)
        )

    def emit(c):
        at = lane(c)
        weight = [w_ref[c, p] for p in range(poles)]

        def body(m, _):
            for half in range(2):
                rows = pl.ds(pl.multiple_of((2 * m + half) * 2 * ROWS, 2 * ROWS), 2 * ROWS)
                near = um_ref[c, rows, :]
                made = []
                for i in range(2):
                    n = 4 * m + 2 * half + i
                    acc = [None] * 4
                    for p in range(poles):
                        term = weight[p] * bcast(s_ref[c, n, pl.ds(p, 1), :])
                        acc[p % 4] = term if acc[p % 4] is None else acc[p % 4] + term
                    total = (acc[0] + acc[1]) + (acc[2] + acc[3])
                    made.append(near[i * ROWS : (i + 1) * ROWS] + mtab[first_in(n)] * total)
                y = jnp.concatenate(made, axis=0)
                out_ref[rows, at] = (q_ref[rows, at].astype(F32) * y).astype(out_ref.dtype)
            return 0

        lax.fori_loop(0, chunks // 4, body, 0)

    for t in range(tiles):
        for copy in loads[t]:
            copy.wait()
        mix(t)
        scan(t)
        if t == 0:
            near = (me > 0).astype(jnp.int32) + (me < last).astype(jnp.int32)
            pl.semaphore_wait(barrier, near)

        @pl.when((me == 0) & (me < last))
        def _():
            pass_on(t).start()

        tails(t)
        hop(0, t)
        serve(t)

    params[1].wait()
    params[2].wait()
    cs_ref[...] = res_ref[...] * jnp.sqrt(1.0 - jnp.exp(-2.0 * rate_ref[...]))
    for t in range(tiles):

        def one(c, _):
            taps(c)
            return 0

        lax.fori_loop(t * per, (t + 1) * per, one, 0)
        if hops > 1:
            hop(1, t)
        serve(tiles + t)

    q_load.wait()
    todo = [(i, t) for i in range(2, hops) for t in range(tiles)]
    for t in range(tiles):
        serve(points + t)

        @pl.when(me > 0)
        def _():
            carry(t)

        for g in range(0, per, 2):
            size = min(2, per - g)

            def one(c, _):
                emit(c)
                return 0

            lax.fori_loop(t * per + g, t * per + g + size, one, 0)
            if t * per + g >= cols // 4 and todo:
                hop(*todo.pop(0))
    for item in todo:
        hop(*item)

    dec_ref[0] = tbuf[source_of(me), :, :]
    for t in range(tiles):
        at = span(t)

        @pl.when(me > 0)
        def _():
            to_right(hops - 1, t).wait_recv()
            dec_ref[0, :, at] = dec_ref[0, :, at] + arr_r[hops - 1, :, at]

        @pl.when(me < last)
        def _():
            to_left(hops - 1, t).wait_recv()
            dec_ref[0, :, at] = dec_ref[0, :, at] + arr_l[hops - 1, :, at]

    for t in range(tiles):

        @pl.when(me < last)
        def _():
            pass_on(t).wait_send()

        for i in range(hops):

            @pl.when((me <= i) & (me < last))
            def _():
                to_right(i, t).wait_send()

            @pl.when((back <= i) & (back < last))
            def _():
                to_left(i, t).wait_send()


def shards(q_feat, k_feat, v_feat, pole_rate, residue, skip_gain, lengths, owners):
    tok, channels = q_feat.shape
    poles, count = pole_rate.shape[0], lengths.shape[0]
    slots = lax.axis_size("ctx")
    cols = channels // LANES
    per = min(4, cols)
    tiles = cols // per
    chunks = tok // ROWS
    hops = max(slots - 1, 1)
    dma = pltpu.SemaphoreType.DMA
    vmem, hbm = pl.BlockSpec(memory_space=pltpu.VMEM), pl.BlockSpec(memory_space=pltpu.HBM)
    smem = pl.BlockSpec(memory_space=pltpu.SMEM)
    state = pltpu.VMEM((poles, channels), F32)
    block = pltpu.VMEM((hops, poles, channels), F32)
    feat = pltpu.VMEM((tok, channels), q_feat.dtype)
    wide = pltpu.VMEM((cols, tok, LANES), F32)
    far = [
        pltpu.with_memory_space_constraint(x, pltpu.HBM)
        for x in (pole_rate, residue, skip_gain[None, :], k_feat, v_feat, q_feat)
    ]
    return pl.pallas_call(
        functools.partial(kernel, tok=tok, poles=poles, count=count, cols=cols, per=per),
        in_specs=[smem] * 2 + [hbm] * 6,
        out_specs=[vmem, vmem],
        out_shape=[
            jax.ShapeDtypeStruct((tok, channels), q_feat.dtype),
            jax.ShapeDtypeStruct((1, poles, channels), F32),
        ],
        scratch_shapes=[
            feat, feat, feat, state, state, pltpu.VMEM((1, channels), F32), wide, wide,
            pltpu.VMEM((cols, chunks + 1, poles, LANES), F32),
            pltpu.VMEM((cols, poles, ROWS, LANES), F32),
            pltpu.VMEM((3, poles, channels), F32),
            pltpu.VMEM((2, poles, channels), F32),
            pltpu.VMEM((3, poles, channels), F32),
            state,
            pltpu.VMEM((ROWS + 1, ROWS, LANES), F32),
            pltpu.VMEM((count, ROWS, LANES), F32),
            pltpu.VMEM((count + 2, poles, channels), F32),
            state, state, block, block, block, block,
            pltpu.SMEM((count,), jnp.int32), pltpu.SMEM((count, ROWS), jnp.int32),
            pltpu.SMEM((count, ROWS), F32),
            dma((3,)), dma((tiles, 2)), dma, dma((tiles,)), dma((tiles,)),
            dma((hops, tiles)), dma((hops, tiles)), dma((hops, tiles)), dma((hops, tiles)),
        ],
        compiler_params=pltpu.CompilerParams(
            collective_id=0, has_side_effects=True, vmem_limit_bytes=40 << 20
        ),
        name="modal",
    )(lengths, owners, *far)


def solution(mesh):
    tokens = P(("groups", "ctx"), "chan")
    return jax.shard_map(
        shards,
        mesh=mesh,
        in_specs=(
            tokens, tokens, tokens, P(None, "chan"), P(None, "chan"), P("chan"),
            P("groups"), P("groups"),
        ),
        out_specs=(tokens, P(("groups", "ctx"), None, "chan")),
        check_vma=False,
    )
```

time: 39.9 us -> 34.5 us (0.86)
  Pallas kernels: 35 us -> 30.4 us
  local copies, waits for them, and re-layouts: 3.85 us -> 3.28 us
    pallas_call x2 -> x1, Pallas kernels: 35 us -> 30.4 us  [shards(): pl.pallas_call(functools.partial(kernel, tok=tok, poles=poles, count=coun...]
    unnamed x4 -> x6, local copies, waits for them, and re-layouts: 3.85 us -> 3.28 us
where the time goes in v1:
time: 34.5 us; the launch traced here: 34.3 us
  Pallas kernels  30.4 us (88%)
  local copies, waits for them, and re-layouts  3.28 us (10%)
  between operations  0.65 us (2%)
    pallas_call x1, Pallas kernels, shards(): pl.pallas_call(functools.partial(kernel, tok=tok, poles=poles, count=coun...  30.4 us
    unnamed x6, local copies, waits for them, and re-layouts  3.28 us

profile of v1, /device:TPU:0, one launch (start us, length us, event | category | flops | bytes accessed | tf_op | source)
XLA Modules:
  0.0 34.3 jit_solution(14469025907774105790)
XLA Ops:
  0.6 0.0 copy-start
  0.6 0.6 %copy-done = s32[4]{0:T(128)S(1)} copy-done((s32[4]{0:T(128)S(1)}, s32[4]{0:T(128)}, u32[]{:S(2)}) %copy-start) | copy-done | bytes 40
  1.3 0.0 copy-start.1
  1.3 0.7 %copy-done.1 = s32[4]{0:T(128)S(1)} copy-done((s32[4]{0:T(128)S(1)}, s32[4]{0:T(128)}, u32[]{:S(2)}) %copy-start.1) | copy-done | bytes 40
  1.9 30.4 %modal.1 = (bf16[512,2048]{1,0:T(8,128)(2,1)S(1)}, f32[1,16,2048]{2,1,0:T(8,128)S(1)}) custom-call(s32[4]{0:T(128)S(1)} %copy-done, s32[4]{0:T(128)S(1)} %copy-done.1, f32[16,2048]{1,0:T(8,128)} %rate_hbm.1, f32[16,2048]{1,0:T(8,128)} %res_hbm.1, f32[1,2048]{1,0:T(1,128)} %bitcast.1, bf16[512,2048]{1,0:T(8,128)(2,1)} %k_hbm.1, bf16[512,2048]{1,0:T(8,128)(2,1)} %v_hbm.1, ...), custom_call_target="tpu_custom_call" | custom-call | tf_op jit(solution)/shard_map/modal/pallas_call | solution.py:502
  32.3 1.3 %copy.12 = bf16[512,2048]{1,0:T(8,128)(2,1)} copy(bf16[512,2048]{1,0:T(8,128)(2,1)S(1)} %get-tuple-element.4) | data formatting | bytes 4194304
  33.7 0.7 %copy.13 = f32[1,16,2048]{2,1,0:T(8,128)} copy(f32[1,16,2048]{2,1,0:T(8,128)S(1)} %get-tuple-element.5) | data formatting | bytes 262144
Async XLA Ops:
  0.6 0.7 %copy-start = (s32[4]{0:T(128)S(1)}, s32[4]{0:T(128)}, u32[]{:S(2)}) copy-start(s32[4]{0:T(128)} %lens_ref.1) | copy-start | bytes 52
  1.3 0.7 %copy-start.1 = (s32[4]{0:T(128)S(1)}, s32[4]{0:T(128)}, u32[]{:S(2)}) copy-start(s32[4]{0:T(128)} %own_ref.1) | copy-start | bytes 52

commit v2 on v1

--- a/solution.py
+++ b/solution.py
@@ -10,6 +10,7 @@
 F32 = jnp.float32
 LANES = 128
 ROWS = 8
+MIX, SCAN, FIR, CARRY, EMIT = 8, 8, 16, 8, 16
 MESH = pl.DeviceIdType.MESH
 
 
@@ -20,12 +21,12 @@
 
 
 def kernel(
-    lens_ref, own_ref, rate_hbm, res_hbm, gain_hbm, k_hbm, v_hbm, q_hbm,
+    lens_hbm, own_hbm, rate_hbm, res_hbm, gain_hbm, k_hbm, v_hbm, q_hbm,
     out_ref, dec_ref,
-    k_ref, v_ref, q_ref, rate_ref, res_ref, gain_ref, u_ref, um_ref, s_ref, w_ref,
-    dtab, etab, ftab, cs_ref, mtab, fix_ref, tbuf,
+    lens_ref, own_ref, k_ref, v_ref, q_ref, rate_ref, res_ref, gain_ref, u_ref, um_ref, s_ref, w_ref,
+    dtab, etab, ftab, cs_ref, mtab, ltab, fix_ref, tbuf,
     arrived, passed, arr_r, put_r, arr_l, put_l,
-    where_ref, kind_ref, inside_ref, par_sem, kv_sem, q_sem, st_send, st_recv, r_send, r_recv, l_send, l_recv,
+    which_ref, where_ref, kind_ref, inside_ref, par_sem, kv_sem, q_sem, st_send, st_recv, r_send, r_recv, l_send, l_recv,
     *, tok, poles, count, cols, per,
 ):
     slots = lax.axis_size("ctx")
@@ -48,10 +49,14 @@
     params = [
         pltpu.make_async_copy(src, dst, par_sem.at[i])
         for i, (src, dst) in enumerate(
-            [(rate_hbm, rate_ref), (res_hbm, res_ref), (gain_hbm, gain_ref)]
+            [
+                (rate_hbm, rate_ref), (res_hbm, res_ref), (gain_hbm, gain_ref),
+                (lens_hbm, lens_ref), (own_hbm, own_ref),
+            ]
         )
     ]
-    params[0].start()
+    for i in (3, 4, 0):
+        params[i].start()
     loads = []
     for t in range(tiles):
         at = pl.ds(t * width, width)
@@ -68,6 +73,8 @@
     q_load = pltpu.make_async_copy(q_hbm, q_ref, q_sem)
     q_load.start()
 
+    params[3].wait()
+    params[4].wait()
     first = me * tok
     offset = jnp.int32(0)
     begin, final = [], []
@@ -82,23 +89,16 @@
     where_in = [lax.shift_right_arithmetic(a, 3) for a in starts]
     rel_in = [lax.bitwise_and(a, ROWS - 1) for a in starts]
 
-    def last_in(n):
-        found = jnp.int32(-1)
-        for chunk, rel in zip(where_in, rel_in):
-            found = jnp.maximum(found, jnp.where(chunk == n, rel, -1))
-        return found
-
-    def first_in(n):
-        found = jnp.int32(ROWS)
-        for chunk, rel in zip(where_in, rel_in):
-            found = jnp.minimum(found, jnp.where(chunk == n, rel, ROWS))
-        return found
-
-    def keeps(n):
-        hit = jnp.int32(1)
-        for chunk in where_in:
-            hit = jnp.where(chunk == n, 0, hit)
-        return hit
+    def mark(m, _):
+        for i in range(4):
+            n = m * 4 + i
+            which = jnp.int32(inner)
+            for x, chunk in enumerate(where_in):
+                which = jnp.where(chunk == n, x, which)
+            which_ref[n] = which
+        return 0
+
+    lax.fori_loop(0, chunks // 4, mark, 0)
 
     covers = jnp.int32(1)
     ends_here, goes_on = [], []
@@ -122,18 +122,26 @@
     def bcast(row):
         return jnp.broadcast_to(row, (ROWS, LANES))
 
-    for n in range(ROWS + 1):
-        mtab[n] = (iota < n).astype(F32)
+    mtab[inner] = jnp.ones((ROWS, LANES), F32)
+    ltab[inner] = jnp.ones((ROWS, LANES), F32)
+    for x, chunk in enumerate(where_in):
+        low, high = jnp.int32(ROWS), jnp.int32(-1)
+        for other, rel in zip(where_in, rel_in):
+            low = jnp.where(other == chunk, jnp.minimum(low, rel), low)
+            high = jnp.where(other == chunk, jnp.maximum(high, rel), high)
+        mtab[x] = jnp.where(iota < low, 1.0, 0.0)
+        ltab[x] = jnp.where(iota >= high, 1.0, 0.0)
     fix_ref[inner] = jnp.zeros((ROWS, LANES), F32)
     tbuf[zero_row] = jnp.zeros(tbuf.shape[1:], F32)
     dtab[0] = jnp.zeros(dtab.shape[1:], F32)
     dtab[2] = jnp.ones(dtab.shape[1:], F32)
-    etab[0] = jnp.zeros(etab.shape[1:], F32)
+    for x in range(inner):
+        etab[x] = jnp.zeros(etab.shape[1:], F32)
     ftab[0] = jnp.zeros(ftab.shape[1:], F32)
     params[0].wait()
     rate = rate_ref[...]
     dtab[1] = jnp.exp(-rate)
-    etab[1] = jnp.exp(rate * -float(ROWS))
+    etab[inner] = jnp.exp(rate * -float(ROWS))
     ftab[1] = jnp.exp(rate * -float(tok))
     ftab[2] = jnp.exp(rate * -dist.astype(F32))
 
@@ -142,31 +150,29 @@
 
     def mix(t):
         def body(m, _):
-            for half in range(2):
-                n = 4 * m + 2 * half
+            for half in range(MIX // 2):
+                n = MIX * m + 2 * half
                 rows = pl.ds(pl.multiple_of(n * ROWS, 2 * ROWS), 2 * ROWS)
-                masks = [iota >= last_in(n + i) for i in range(2)]
+                masks = [ltab[which_ref[n + i]] for i in range(2)]
                 for c in range(t * per, (t + 1) * per):
                     u = k_ref[rows, lane(c)].astype(F32) * v_ref[rows, lane(c)].astype(F32)
                     u_ref[c, rows, :] = u
                     for i in range(2):
                         at = pl.ds(pl.multiple_of((n + i) * ROWS, ROWS), ROWS)
-                        um_ref[c, at, :] = jnp.where(
-                            masks[i], u[i * ROWS : (i + 1) * ROWS], 0.0
-                        )
+                        um_ref[c, at, :] = u[i * ROWS : (i + 1) * ROWS] * masks[i]
             return 0
 
-        lax.fori_loop(0, chunks // 4, body, 0)
+        lax.fori_loop(0, chunks // MIX, body, 0)
 
     def scan(t):
         pairs = [(c, h) for c in range(t * per, (t + 1) * per) for h in range(halves)]
 
         def body(m, state):
             state = list(state)
-            for i in range(4):
-                n = 4 * m + i
+            for i in range(SCAN):
+                n = SCAN * m + i
                 base = n * ROWS
-                keep = keeps(n)
+                keep = which_ref[n]
                 for x, (c, h) in enumerate(pairs):
                     s_ref[c, n, part(h), :] = state[x]
                 local = [None] * len(pairs)
@@ -185,7 +191,7 @@
             return tuple(state)
 
         zero = jnp.zeros((ROWS, LANES), F32)
-        state = lax.fori_loop(0, chunks // 4, body, tuple(zero for _ in pairs))
+        state = lax.fori_loop(0, chunks // SCAN, body, tuple(zero for _ in pairs))
         for x, (c, h) in enumerate(pairs):
             s_ref[c, chunks, part(h), :] = state[x]
             tbuf[count, part(h), lane(c)] = state[x] * ftab[2, part(h), lane(c)]
@@ -341,35 +347,32 @@
             fix_ref[x] = value
 
         def body(m, _):
-            for i in range(4):
-                n = m * 4 + i
-                which = jnp.int32(inner)
-                for x, chunk in enumerate(where_in):
-                    which = jnp.where(chunk == n, x, which)
-                acc = [fix_ref[which], None]
+            for i in range(FIR):
+                n = m * FIR + i
+                acc = [fix_ref[which_ref[n]], None]
                 for j in range(ROWS):
                     term = taps[j] * bcast(u_ref[c, pl.ds(n * ROWS + j, 1), :])
                     acc[j % 2] = term if acc[j % 2] is None else acc[j % 2] + term
                 um_ref[c, pl.ds(pl.multiple_of(n * ROWS, ROWS), ROWS), :] = acc[0] + acc[1]
             return 0
 
-        lax.fori_loop(0, chunks // 4, body, 0)
+        lax.fori_loop(0, chunks // FIR, body, 0)
 
     def carry(t):
         pairs = [(c, h) for c in range(t * per, (t + 1) * per) for h in range(halves)]
 
         def body(m, state):
             state = list(state)
-            for i in range(4):
-                n = m * 4 + i
-                keep = keeps(n)
+            for i in range(CARRY):
+                n = m * CARRY + i
+                keep = which_ref[n]
                 for x, (c, h) in enumerate(pairs):
                     s_ref[c, n, part(h), :] = s_ref[c, n, part(h), :] + state[x]
                     state[x] = etab[keep, part(h), lane(c)] * state[x]
             return tuple(state)
 
         lax.fori_loop(
-            0, chunks // 4, body, tuple(arrived[part(h), lane(c)] for c, h in pairs)
+            0, chunks // CARRY, body, tuple(arrived[part(h), lane(c)] for c, h in pairs)
         )
 
     def emit(c):
@@ -377,23 +380,24 @@
         weight = [w_ref[c, p] for p in range(poles)]
 
         def body(m, _):
-            for half in range(2):
-                rows = pl.ds(pl.multiple_of((2 * m + half) * 2 * ROWS, 2 * ROWS), 2 * ROWS)
+            for half in range(EMIT // 2):
+                first_row = (EMIT * m + 2 * half) * ROWS
+                rows = pl.ds(pl.multiple_of(first_row, 2 * ROWS), 2 * ROWS)
                 near = um_ref[c, rows, :]
                 made = []
                 for i in range(2):
-                    n = 4 * m + 2 * half + i
+                    n = EMIT * m + 2 * half + i
                     acc = [None] * 4
                     for p in range(poles):
                         term = weight[p] * bcast(s_ref[c, n, pl.ds(p, 1), :])
                         acc[p % 4] = term if acc[p % 4] is None else acc[p % 4] + term
                     total = (acc[0] + acc[1]) + (acc[2] + acc[3])
-                    made.append(near[i * ROWS : (i + 1) * ROWS] + mtab[first_in(n)] * total)
+                    made.append(near[i * ROWS : (i + 1) * ROWS] + mtab[which_ref[n]] * total)
                 y = jnp.concatenate(made, axis=0)
                 out_ref[rows, at] = (q_ref[rows, at].astype(F32) * y).astype(out_ref.dtype)
             return 0
 
-        lax.fori_loop(0, chunks // 4, body, 0)
+        lax.fori_loop(0, chunks // EMIT, body, 0)
 
     for t in range(tiles):
         for copy in loads[t]:
@@ -490,45 +494,47 @@
     hops = max(slots - 1, 1)
     dma = pltpu.SemaphoreType.DMA
     vmem, hbm = pl.BlockSpec(memory_space=pltpu.VMEM), pl.BlockSpec(memory_space=pltpu.HBM)
-    smem = pl.BlockSpec(memory_space=pltpu.SMEM)
     state = pltpu.VMEM((poles, channels), F32)
+    small = pltpu.VMEM((count, ROWS, LANES), F32)
     block = pltpu.VMEM((hops, poles, channels), F32)
     feat = pltpu.VMEM((tok, channels), q_feat.dtype)
     wide = pltpu.VMEM((cols, tok, LANES), F32)
-    far = [
+    args = [
         pltpu.with_memory_space_constraint(x, pltpu.HBM)
-        for x in (pole_rate, residue, skip_gain[None, :], k_feat, v_feat, q_feat)
+        for x in (
+            lengths, owners, pole_rate, residue, skip_gain[None, :], k_feat, v_feat, q_feat
+        )
     ]
     return pl.pallas_call(
         functools.partial(kernel, tok=tok, poles=poles, count=count, cols=cols, per=per),
-        in_specs=[smem] * 2 + [hbm] * 6,
+        in_specs=[hbm] * 8,
         out_specs=[vmem, vmem],
         out_shape=[
             jax.ShapeDtypeStruct((tok, channels), q_feat.dtype),
             jax.ShapeDtypeStruct((1, poles, channels), F32),
         ],
         scratch_shapes=[
+            pltpu.SMEM((count,), jnp.int32), pltpu.SMEM((count,), jnp.int32),
             feat, feat, feat, state, state, pltpu.VMEM((1, channels), F32), wide, wide,
             pltpu.VMEM((cols, chunks + 1, poles, LANES), F32),
             pltpu.VMEM((cols, poles, ROWS, LANES), F32),
             pltpu.VMEM((3, poles, channels), F32),
-            pltpu.VMEM((2, poles, channels), F32),
+            pltpu.VMEM((count, poles, channels), F32),
             pltpu.VMEM((3, poles, channels), F32),
             state,
-            pltpu.VMEM((ROWS + 1, ROWS, LANES), F32),
-            pltpu.VMEM((count, ROWS, LANES), F32),
+            small, small, small,
             pltpu.VMEM((count + 2, poles, channels), F32),
             state, state, block, block, block, block,
-            pltpu.SMEM((count,), jnp.int32), pltpu.SMEM((count, ROWS), jnp.int32),
+            pltpu.SMEM((chunks,), jnp.int32), pltpu.SMEM((count,), jnp.int32), pltpu.SMEM((count, ROWS), jnp.int32),
             pltpu.SMEM((count, ROWS), F32),
-            dma((3,)), dma((tiles, 2)), dma, dma((tiles,)), dma((tiles,)),
+            dma((5,)), dma((tiles, 2)), dma, dma((tiles,)), dma((tiles,)),
             dma((hops, tiles)), dma((hops, tiles)), dma((hops, tiles)), dma((hops, tiles)),
         ],
         compiler_params=pltpu.CompilerParams(
             collective_id=0, has_side_effects=True, vmem_limit_bytes=40 << 20
         ),
         name="modal",
-    )(lengths, owners, *far)
+    )(*args)
 
 
 def solution(mesh):

time: 34.5 us -> 26.2 us (0.76)
  the two profiles are of different devices: /device:TPU:0 before, /device:TPU:12 now
where the time goes in v2:
time: 26.2 us; the launch traced here: 26.1 us
  Pallas kernels  23.5 us (90%)
  local copies, waits for them, and re-layouts  1.98 us (8%)
  between operations  0.64 us (2%)
    pallas_call x1, Pallas kernels, shards(): pl.pallas_call(functools.partial(kernel, tok=tok, poles=poles, count=coun...  23.5 us
    unnamed x2, local copies, waits for them, and re-layouts  1.98 us

profile of v2, /device:TPU:12, one launch (start us, length us, event | category | flops | bytes accessed | tf_op | source)
XLA Modules:
  0.0 26.1 jit_solution(12283099645609596870)
XLA Ops:
  0.6 23.5 %modal.1 = (bf16[512,2048]{1,0:T(8,128)(2,1)S(1)}, f32[1,16,2048]{2,1,0:T(8,128)S(1)}) custom-call(s32[4]{0:T(128)} %lens_hbm.1, s32[4]{0:T(128)} %own_hbm.1, f32[16,2048]{1,0:T(8,128)} %rate_hbm.1, f32[16,2048]{1,0:T(8,128)} %res_hbm.1, f32[1,2048]{1,0:T(1,128)} %bitcast.1, bf16[512,2048]{1,0:T(8,128)(2,1)} %k_hbm.1, bf16[512,2048]{1,0:T(8,128)(2,1)} %v_hbm.1, ...), custom_call_target="tpu_custom_call" | custom-call | tf_op jit(solution)/shard_map/modal/pallas_call | solution.py:508
  24.1 1.3 %copy.12 = bf16[512,2048]{1,0:T(8,128)(2,1)} copy(bf16[512,2048]{1,0:T(8,128)(2,1)S(1)} %get-tuple-element.4) | data formatting | bytes 4194304
  25.4 0.7 %copy.13 = f32[1,16,2048]{2,1,0:T(8,128)} copy(f32[1,16,2048]{2,1,0:T(8,128)S(1)} %get-tuple-element.5) | data formatting | bytes 262144

commit v3 on v2

--- a/solution.py
+++ b/solution.py
@@ -11,6 +11,8 @@
 LANES = 128
 ROWS = 8
 MIX, SCAN, FIR, CARRY, EMIT = 8, 8, 16, 8, 16
+START, SCAN_US, TAPS_US, CARRY_US, EMIT_US = 1.2, 0.43, 0.23, 0.06, 0.36
+LINK_US, WIRE_US, QUEUE_US = 0.0105, 2.0, 0.1
 MESH = pl.DeviceIdType.MESH
 
 
@@ -38,13 +40,10 @@
     width = per * LANES
     barrier = pltpu.get_barrier_semaphore()
 
-    @pl.when(me > 0)
-    def _():
-        pl.semaphore_signal(barrier, inc=1, device_id={"ctx": me - 1}, device_id_type=MESH)
-
-    @pl.when(me < last)
-    def _():
-        pl.semaphore_signal(barrier, inc=1, device_id={"ctx": me + 1}, device_id_type=MESH)
+    for j in range(1, slots):
+        pl.semaphore_signal(
+            barrier, inc=1, device_id={"ctx": lax.rem(me + j, slots)}, device_id_type=MESH
+        )
 
     params = [
         pltpu.make_async_copy(src, dst, par_sem.at[i])
@@ -191,7 +190,10 @@
             return tuple(state)
 
         zero = jnp.zeros((ROWS, LANES), F32)
-        state = lax.fori_loop(0, chunks // SCAN, body, tuple(zero for _ in pairs))
+        steps = chunks // SCAN
+        state = lax.fori_loop(0, steps // 2, body, tuple(zero for _ in pairs))
+        serve("half", t)
+        state = lax.fori_loop(steps // 2, steps, body, state)
         for x, (c, h) in enumerate(pairs):
             s_ref[c, chunks, part(h), :] = state[x]
             tbuf[count, part(h), lane(c)] = state[x] * ftab[2, part(h), lane(c)]
@@ -264,60 +266,103 @@
             device_id={"ctx": me + 1}, device_id_type=MESH,
         )
 
-    def to_left(i, t):
+    def to_left(gap, t):
         return pltpu.make_async_remote_copy(
-            src_ref=put_l.at[i, :, span(t)], dst_ref=arr_l.at[i, :, span(t)],
-            send_sem=l_send.at[i, t], recv_sem=l_recv.at[i, t],
-            device_id={"ctx": me - 1}, device_id_type=MESH,
-        )
-
-    back = last - me
-
-    def hop(i, t):
+            src_ref=put_l.at[gap - 1, :, span(t)], dst_ref=arr_l.at[gap - 1, :, span(t)],
+            send_sem=l_send.at[gap - 1, t], recv_sem=l_recv.at[gap - 1, t],
+            device_id={"ctx": me - gap}, device_id_type=MESH,
+        )
+
+    def give_left(t):
+        for gap in range(last, 0, -1):
+
+            @pl.when(me >= gap)
+            def _():
+                put_l[gap - 1, :, span(t)] = tbuf[source_of(me - gap), :, span(t)]
+                to_left(gap, t).start()
+
+    def hop(m, i, t):
         at = span(t)
 
-        @pl.when((me <= i) & (me < last))
+        @pl.when(me == m)
         def _():
-            own = tbuf[source_of(me + last - i), :, at]
+            own = tbuf[source_of(m + last - i), :, at]
+            if m:
+                to_right(i - 1, t).wait_recv()
+                own = own + arr_r[i - 1, :, at]
             put_r[i, :, at] = own
-            if i:
-
-                @pl.when(me > 0)
-                def _():
-                    to_right(i - 1, t).wait_recv()
-                    put_r[i, :, at] = own + arr_r[i - 1, :, at]
-
             to_right(i, t).start()
 
-        @pl.when((back <= i) & (back < last))
-        def _():
-            own = tbuf[source_of(i - back), :, at]
-            put_l[i, :, at] = own
-            if i:
-
-                @pl.when(back > 0)
-                def _():
-                    to_left(i - 1, t).wait_recv()
-                    put_l[i, :, at] = own + arr_l[i - 1, :, at]
-
-            to_left(i, t).start()
-
     hops = last
-    points = 2 * tiles
-    lag = 2
-
-    def serve(point):
-        for t in range(tiles):
-            if point < points:
-                due = (me > 0) & (t + lag * me == point)
-            elif t == point - points:
-                due = (me > 0) & (t + lag * me >= points)
+    group = 2 if per % 2 == 0 else 1
+    names, clock, now = [], {}, START
+    for t in range(tiles):
+        for name in (("half", t), ("scan", t)):
+            now += SCAN_US * per / 2
+            names.append(name)
+            clock[name] = now
+    for g in range(cols // group):
+        now += TAPS_US * group
+        names.append(("taps", g))
+        clock[names[-1]] = now
+    for g in range(cols // group):
+        if g * group % per == 0:
+            names.append(("carry", g * group // per))
+            clock[names[-1]] = now
+            now += CARRY_US * per
+        now += EMIT_US * group
+        names.append(("emit", g))
+        clock[names[-1]] = now
+    jobs = {name: [] for name in names}
+    send_us = LINK_US * per * poles
+    free, reach, open_jobs = [0.0] * slots, {}, []
+    for t in range(tiles):
+        open_jobs += [("relay", m, 0, t) for m in range(1, slots)]
+        open_jobs += [("hop", m, i, t) for i in range(hops) for m in range(i + 1)]
+    open_jobs.sort(key=lambda job: (job[0] == "hop", job[2], job[3]))
+
+    def ship(m, now):
+        free[m] = max(free[m], now) + send_us
+        return free[m] + WIRE_US
+
+    scanned = set()
+    for name in names:
+        now = clock[name]
+        later = min([clock[x] for x in names if clock[x] > now] or [now]) + QUEUE_US
+        if name[0] == "scan":
+            scanned.add(name[1])
+            reach["relay", 1, 0, name[1]] = ship(0, now)
+        for job in list(open_jobs):
+            kind, m, i, t = job
+            if t not in scanned:
+                continue
+            if kind == "relay":
+                ready = reach.get(job, 1e9) <= now and m < last
+                ready = ready or name == ("carry", t)
             else:
-                continue
-
-            @pl.when(due)
+                ready = (m == 0 or reach.get(("hop", m, i, t), 1e9) <= now)
+                ready = ready and free[m] <= later
+            if ready:
+                jobs[name].append(job)
+                open_jobs.remove(job)
+                if m < last:
+                    after = (kind, m + 1, i + 1 if kind == "hop" else 0, t)
+                    reach[after] = ship(m, now)
+    open_jobs.sort(key=lambda job: job[2])
+
+    def run(job):
+        kind, m, i, t = job
+        if kind == "hop":
+            hop(m, i, t)
+        else:
+
+            @pl.when(me == m)
             def _():
                 relay(t)
+
+    def serve(*name):
+        for job in jobs[name]:
+            run(job)
 
     def taps(c):
         at = lane(c)
@@ -405,52 +450,45 @@
         mix(t)
         scan(t)
         if t == 0:
-            near = (me > 0).astype(jnp.int32) + (me < last).astype(jnp.int32)
-            pl.semaphore_wait(barrier, near)
+            pl.semaphore_wait(barrier, last)
 
         @pl.when((me == 0) & (me < last))
         def _():
             pass_on(t).start()
 
         tails(t)
-        hop(0, t)
-        serve(t)
+        give_left(t)
+        serve("scan", t)
 
     params[1].wait()
     params[2].wait()
     cs_ref[...] = res_ref[...] * jnp.sqrt(1.0 - jnp.exp(-2.0 * rate_ref[...]))
-    for t in range(tiles):
-
+
+    def each(step, g):
         def one(c, _):
-            taps(c)
+            step(c)
             return 0
 
-        lax.fori_loop(t * per, (t + 1) * per, one, 0)
-        if hops > 1:
-            hop(1, t)
-        serve(tiles + t)
-
+        lax.fori_loop(g * group, (g + 1) * group, one, 0)
+
+    for g in range(cols // group):
+        each(taps, g)
+        serve("taps", g)
     q_load.wait()
-    todo = [(i, t) for i in range(2, hops) for t in range(tiles)]
-    for t in range(tiles):
-        serve(points + t)
-
-        @pl.when(me > 0)
-        def _():
-            carry(t)
-
-        for g in range(0, per, 2):
-            size = min(2, per - g)
-
-            def one(c, _):
-                emit(c)
-                return 0
-
-            lax.fori_loop(t * per + g, t * per + g + size, one, 0)
-            if t * per + g >= cols // 4 and todo:
-                hop(*todo.pop(0))
-    for item in todo:
-        hop(*item)
+    for g in range(cols // group):
+        if g * group % per == 0:
+            t = g * group // per
+            serve("carry", t)
+
+            @pl.when(me > 0)
+            def _():
+                carry(t)
+
+        each(emit, g)
+        serve("emit", g)
+
+    for job in open_jobs:
+        run(job)
 
     dec_ref[0] = tbuf[source_of(me), :, :]
     for t in range(tiles):
@@ -461,10 +499,12 @@
             to_right(hops - 1, t).wait_recv()
             dec_ref[0, :, at] = dec_ref[0, :, at] + arr_r[hops - 1, :, at]
 
-        @pl.when(me < last)
-        def _():
-            to_left(hops - 1, t).wait_recv()
-            dec_ref[0, :, at] = dec_ref[0, :, at] + arr_l[hops - 1, :, at]
+        for gap in range(1, slots):
+
+            @pl.when(me + gap <= last)
+            def _():
+                to_left(gap, t).wait_recv()
+                dec_ref[0, :, at] = dec_ref[0, :, at] + arr_l[gap - 1, :, at]
 
     for t in range(tiles):
 
@@ -478,9 +518,9 @@
             def _():
                 to_right(i, t).wait_send()
 
-            @pl.when((back <= i) & (back < last))
-            def _():
-                to_left(i, t).wait_send()
+            @pl.when(me > i)
+            def _():
+                to_left(i + 1, t).wait_send()
 
 
 def shards(q_feat, k_feat, v_feat, pole_rate, residue, skip_gain, lengths, owners):

time: 26.2 us -> 23.1 us (0.88)
  the two profiles are of different devices: /device:TPU:12 before, /device:TPU:0 now
where the time goes in v3:
time: 23.1 us; the launch traced here: 22.8 us
  Pallas kernels  20.2 us (87%)
  local copies, waits for them, and re-layouts  1.98 us (9%)
  between operations  0.64 us (3%)
    pallas_call x1, Pallas kernels, shards(): pl.pallas_call(functools.partial(kernel, tok=tok, poles=poles, count=coun...  20.2 us
    unnamed x2, local copies, waits for them, and re-layouts  1.98 us

profile of v3, /device:TPU:0, one launch (start us, length us, event | category | flops | bytes accessed | tf_op | source)
XLA Modules:
  0.0 22.8 jit_solution(14058604914094011690)
XLA Ops:
  0.6 20.2 %modal.1 = (bf16[512,2048]{1,0:T(8,128)(2,1)S(1)}, f32[1,16,2048]{2,1,0:T(8,128)S(1)}) custom-call(s32[4]{0:T(128)} %lens_hbm.1, s32[4]{0:T(128)} %own_hbm.1, f32[16,2048]{1,0:T(8,128)} %rate_hbm.1, f32[16,2048]{1,0:T(8,128)} %res_hbm.1, f32[1,2048]{1,0:T(1,128)} %bitcast.1, bf16[512,2048]{1,0:T(8,128)(2,1)} %k_hbm.1, bf16[512,2048]{1,0:T(8,128)(2,1)} %v_hbm.1, ...), custom_call_target="tpu_custom_call" | custom-call | tf_op jit(solution)/shard_map/modal/pallas_call | solution.py:548
  20.8 1.3 %copy.12 = bf16[512,2048]{1,0:T(8,128)(2,1)} copy(bf16[512,2048]{1,0:T(8,128)(2,1)S(1)} %get-tuple-element.4) | data formatting | bytes 4194304
  22.1 0.7 %copy.13 = f32[1,16,2048]{2,1,0:T(8,128)} copy(f32[1,16,2048]{2,1,0:T(8,128)S(1)} %get-tuple-element.5) | data formatting | bytes 262144

commit v4 on v3

--- a/solution.py
+++ b/solution.py
@@ -22,19 +22,78 @@
     return pl.ds(pl.multiple_of(c * LANES, LANES), LANES)
 
 
+def produce(mask, w_ref, s_ref, near_ref, q_ref, out_ref, at, poles, chunks):
+    weight = [w_ref[p] for p in range(poles)]
+
+    def body(m, _):
+        for half in range(EMIT // 2):
+            first_row = (EMIT * m + 2 * half) * ROWS
+            rows = pl.ds(pl.multiple_of(first_row, 2 * ROWS), 2 * ROWS)
+            near = near_ref[rows, :]
+            made = []
+            for i in range(2):
+                n = EMIT * m + 2 * half + i
+                acc = [None] * 4
+                for p in range(poles):
+                    term = weight[p] * jnp.broadcast_to(s_ref[n, pl.ds(p, 1), :], (ROWS, LANES))
+                    acc[p % 4] = term if acc[p % 4] is None else acc[p % 4] + term
+                total = (acc[0] + acc[1]) + (acc[2] + acc[3])
+                made.append(near[i * ROWS : (i + 1) * ROWS] + mask(n) * total)
+            y = jnp.concatenate(made, axis=0)
+            out_ref[rows, at] = (q_ref[rows, at].astype(F32) * y).astype(out_ref.dtype)
+        return 0
+
+    lax.fori_loop(0, chunks // EMIT, body, 0)
+
+
+def finish(dec_ref, s_ref, near_ref, w_ref, q_ref, mask_ref, *rest, poles, chunks, per, ahead):
+    rest = list(rest)
+    head_ref = rest.pop(0) if ahead else None
+    out_hbm, dec_hbm, made_ref, sem = rest
+    copies = [pltpu.make_async_copy(dec_ref, dec_hbm, sem.at[0])]
+    edge = ahead * per * LANES
+    if ahead:
+        copies.append(pltpu.make_async_copy(head_ref, out_hbm.at[:, pl.ds(0, edge)], sem.at[1]))
+    for copy in copies:
+        copy.start()
+    for c in range(per):
+        produce(
+            lambda n: mask_ref[n], w_ref.at[c], s_ref.at[c], near_ref.at[c],
+            q_ref, made_ref, lane(c), poles, chunks,
+        )
+        copies.append(
+            pltpu.make_async_copy(
+                made_ref.at[:, lane(c)],
+                out_hbm.at[:, pl.ds(edge + c * LANES, LANES)], sem.at[2 + c],
+            )
+        )
+        copies[-1].start()
+    for copy in copies:
+        copy.wait()
+
+
 def kernel(
     lens_hbm, own_hbm, rate_hbm, res_hbm, gain_hbm, k_hbm, v_hbm, q_hbm,
-    out_ref, dec_ref,
-    lens_ref, own_ref, k_ref, v_ref, q_ref, rate_ref, res_ref, gain_ref, u_ref, um_ref, s_ref, w_ref,
-    dtab, etab, ftab, cs_ref, mtab, ltab, fix_ref, tbuf,
-    arrived, passed, arr_r, put_r, arr_l, put_l,
-    which_ref, where_ref, kind_ref, inside_ref, par_sem, kv_sem, q_sem, st_send, st_recv, r_send, r_recv, l_send, l_recv,
-    *, tok, poles, count, cols, per,
+    dec_ref, s_out, um_out, w_out, qt_ref, mask_ref, *rest,
+    tok, poles, count, cols, per,
 ):
+    tiles = cols // per
+    ahead = tiles - 1
+    rest = list(rest)
+    out_ref, q_ref = (rest.pop(0), rest.pop(0)) if ahead else (None, None)
+    s_all = [rest.pop(0) for _ in range(ahead)] + [s_out]
+    um_all = [rest.pop(0) for _ in range(ahead)] + [um_out]
+    w_all = [rest.pop(0) for _ in range(ahead)] + [w_out]
+    (
+        lens_ref, own_ref, k_ref, v_ref, rate_ref, res_ref, gain_ref, u_ref,
+        dtab, etab, ftab, cs_ref, mtab, ltab, fix_ref, tbuf,
+        arrived, passed, arr_r, put_r, arr_l, put_l,
+        which_ref, where_ref, kind_ref, inside_ref,
+        par_sem, kv_sem, q_sem, st_send, st_recv, r_send, r_recv, l_send, l_recv,
+    ) = rest
     slots = lax.axis_size("ctx")
     last = slots - 1
     me = lax.axis_index("ctx")
-    tiles = cols // per
     halves = poles // ROWS
     chunks = tok // ROWS
     width = per * LANES
@@ -69,8 +128,14 @@
             copy.start()
     params[1].start()
     params[2].start()
-    q_load = pltpu.make_async_copy(q_hbm, q_ref, q_sem)
-    q_load.start()
+    edge = ahead * width
+    q_loads = [pltpu.make_async_copy(q_hbm.at[:, pl.ds(edge, width)], qt_ref, q_sem.at[0])]
+    if ahead:
+        q_loads.append(
+            pltpu.make_async_copy(q_hbm.at[:, pl.ds(0, edge)], q_ref, q_sem.at[1])
+        )
+    for copy in q_loads:
+        copy.start()
 
     params[3].wait()
     params[4].wait()
@@ -112,7 +177,8 @@
     def source_of(slot):
         row = jnp.int32(zero_row)
         for r in range(count):
-            kind = jnp.where(ends_here[r], r, jnp.where(goes_on[r], count, zero_row))
+            kind = r if r < count - 1 else count
+            kind = jnp.where(ends_here[r], kind, jnp.where(goes_on[r], count, zero_row))
             row = jnp.where(own_ref[r] == slot, kind, row)
         return row
 
@@ -130,6 +196,13 @@
             high = jnp.where(other == chunk, jnp.maximum(high, rel), high)
         mtab[x] = jnp.where(iota < low, 1.0, 0.0)
         ltab[x] = jnp.where(iota >= high, 1.0, 0.0)
+
+    def cover(m, _):
+        for i in range(8):
+            mask_ref[m * 8 + i] = mtab[which_ref[m * 8 + i]]
+        return 0
+
+    lax.fori_loop(0, chunks // 8, cover, 0)
     fix_ref[inner] = jnp.zeros((ROWS, LANES), F32)
     tbuf[zero_row] = jnp.zeros(tbuf.shape[1:], F32)
     dtab[0] = jnp.zeros(dtab.shape[1:], F32)
@@ -158,7 +231,7 @@
                     u_ref[c, rows, :] = u
                     for i in range(2):
                         at = pl.ds(pl.multiple_of((n + i) * ROWS, ROWS), ROWS)
-                        um_ref[c, at, :] = u[i * ROWS : (i + 1) * ROWS] * masks[i]
+                        um_all[t][c - t * per, at, :] = u[i * ROWS : (i + 1) * ROWS] * masks[i]
             return 0
 
         lax.fori_loop(0, chunks // MIX, body, 0)
@@ -173,11 +246,11 @@
                 base = n * ROWS
                 keep = which_ref[n]
                 for x, (c, h) in enumerate(pairs):
-                    s_ref[c, n, part(h), :] = state[x]
+                    s_all[t][c - t * per, n, part(h), :] = state[x]
                 local = [None] * len(pairs)
                 for j in range(ROWS):
                     rows = {
-                        c: bcast(um_ref[c, pl.ds(base + j, 1), :])
+                        c: bcast(um_all[t][c - t * per, pl.ds(base + j, 1), :])
                         for c in range(t * per, (t + 1) * per)
                     }
                     for x, (c, h) in enumerate(pairs):
@@ -195,14 +268,14 @@
         serve("half", t)
         state = lax.fori_loop(steps // 2, steps, body, state)
         for x, (c, h) in enumerate(pairs):
-            s_ref[c, chunks, part(h), :] = state[x]
+            s_all[t][c - t * per, chunks, part(h), :] = state[x]
             tbuf[count, part(h), lane(c)] = state[x] * ftab[2, part(h), lane(c)]
 
             @pl.when(me == 0)
             def _():
                 passed[part(h), lane(c)] = state[x]
 
-    for r in range(count):
+    for r in range(count - 1):
         end = jnp.clip(final[r], 0, tok - 1)
         n = lax.shift_right_logical(end, 3)
         stop = end - n * ROWS
@@ -215,12 +288,12 @@
             inside_ref[r, j] = jnp.where(inside, 1.0, 0.0).astype(F32)
 
     def tails(t):
-        for r in range(count):
+        for r in range(count - 1):
             n = where_ref[r]
             kinds = [kind_ref[r, j] for j in range(ROWS)]
             weights = [inside_ref[r, j] for j in range(ROWS)]
             for c in range(t * per, (t + 1) * per):
-                value = [s_ref[c, n, part(h), :] for h in range(halves)]
+                value = [s_all[t][c - t * per, n, part(h), :] for h in range(halves)]
                 for j in range(ROWS):
                     row = bcast(u_ref[c, pl.ds(n * ROWS + j, 1), :]) * weights[j]
                     value = [
@@ -254,7 +327,7 @@
             for c in range(t * per, (t + 1) * per):
                 for h in range(halves):
                     passed[part(h), lane(c)] = (
-                        s_ref[c, chunks, part(h), :]
+                        s_all[t][c - t * per, chunks, part(h), :]
                         + ftab[covers, part(h), lane(c)] * arrived[part(h), lane(c)]
                     )
             pass_on(t).start()
@@ -310,7 +383,7 @@
             names.append(("carry", g * group // per))
             clock[names[-1]] = now
             now += CARRY_US * per
-        now += EMIT_US * group
+        now += EMIT_US * group if g * group < (tiles - 1) * per else 0.0
         names.append(("emit", g))
         clock[names[-1]] = now
     jobs = {name: [] for name in names}
@@ -364,7 +437,7 @@
         for job in jobs[name]:
             run(job)
 
-    def taps(c):
+    def taps(t, c):
         at = lane(c)
         steps = (iota + 1).astype(F32)
         total = jnp.zeros((ROWS, LANES), F32)
@@ -372,7 +445,7 @@
         for p in range(poles):
             scale = bcast(cs_ref[pl.ds(p, 1), at])
             value = scale * jnp.exp(bcast(rate_ref[pl.ds(p, 1), at]) * -steps)
-            w_ref[c, p] = value
+            w_all[t][c - t * per, p] = value
             total = total + value
             head = head + scale
         lead = jnp.where(iota == 0, head, pltpu.roll(total, 1, 0))
@@ -398,7 +471,7 @@
                 for j in range(ROWS):
                     term = taps[j] * bcast(u_ref[c, pl.ds(n * ROWS + j, 1), :])
                     acc[j % 2] = term if acc[j % 2] is None else acc[j % 2] + term
-                um_ref[c, pl.ds(pl.multiple_of(n * ROWS, ROWS), ROWS), :] = acc[0] + acc[1]
+                um_all[t][c - t * per, pl.ds(pl.multiple_of(n * ROWS, ROWS), ROWS), :] = acc[0] + acc[1]
             return 0
 
         lax.fori_loop(0, chunks // FIR, body, 0)
@@ -412,7 +485,7 @@
                 n = m * CARRY + i
                 keep = which_ref[n]
                 for x, (c, h) in enumerate(pairs):
-                    s_ref[c, n, part(h), :] = s_ref[c, n, part(h), :] + state[x]
+                    s_all[t][c - t * per, n, part(h), :] = s_all[t][c - t * per, n, part(h), :] + state[x]
                     state[x] = etab[keep, part(h), lane(c)] * state[x]
             return tuple(state)
 
@@ -420,29 +493,12 @@
             0, chunks // CARRY, body, tuple(arrived[part(h), lane(c)] for c, h in pairs)
         )
 
-    def emit(c):
-        at = lane(c)
-        weight = [w_ref[c, p] for p in range(poles)]
-
-        def body(m, _):
-            for half in range(EMIT // 2):
-                first_row = (EMIT * m + 2 * half) * ROWS
-                rows = pl.ds(pl.multiple_of(first_row, 2 * ROWS), 2 * ROWS)
-                near = um_ref[c, rows, :]
-                made = []
-                for i in range(2):
-                    n = EMIT * m + 2 * half + i
-                    acc = [None] * 4
-                    for p in range(poles):
-                        term = weight[p] * bcast(s_ref[c, n, pl.ds(p, 1), :])
-                        acc[p % 4] = term if acc[p % 4] is None else acc[p % 4] + term
-                    total = (acc[0] + acc[1]) + (acc[2] + acc[3])
-                    made.append(near[i * ROWS : (i + 1) * ROWS] + mtab[which_ref[n]] * total)
-                y = jnp.concatenate(made, axis=0)
-                out_ref[rows, at] = (q_ref[rows, at].astype(F32) * y).astype(out_ref.dtype)
-            return 0
-
-        lax.fori_loop(0, chunks // EMIT, body, 0)
+    def emit(t, c):
+        local = c - t * per
+        produce(
+            lambda n: mtab[which_ref[n]], w_all[t].at[local], s_all[t].at[local],
+            um_all[t].at[local], q_ref, out_ref, lane(c), poles, chunks,
+        )
 
     for t in range(tiles):
         for copy in loads[t]:
@@ -466,7 +522,7 @@
 
     def each(step, g):
         def one(c, _):
-            step(c)
+            step(g * group // per, c)
             return 0
 
         lax.fori_loop(g * group, (g + 1) * group, one, 0)
@@ -474,7 +530,8 @@
     for g in range(cols // group):
         each(taps, g)
         serve("taps", g)
-    q_load.wait()
+    for copy in q_loads:
+        copy.wait()
     for g in range(cols // group):
         if g * group % per == 0:
             t = g * group // per
@@ -484,7 +541,8 @@
             def _():
                 carry(t)
 
-        each(emit, g)
+        if g * group < ahead * per:
+            each(emit, g)
         serve("emit", g)
 
     for job in open_jobs:
@@ -534,30 +592,46 @@
     hops = max(slots - 1, 1)
     dma = pltpu.SemaphoreType.DMA
     vmem, hbm = pl.BlockSpec(memory_space=pltpu.VMEM), pl.BlockSpec(memory_space=pltpu.HBM)
+    ahead = tiles - 1
+    width = per * LANES
+    edge = ahead * width
     state = pltpu.VMEM((poles, channels), F32)
     small = pltpu.VMEM((count, ROWS, LANES), F32)
     block = pltpu.VMEM((hops, poles, channels), F32)
     feat = pltpu.VMEM((tok, channels), q_feat.dtype)
-    wide = pltpu.VMEM((cols, tok, LANES), F32)
+    s_shape, near_shape = (per, chunks + 1, poles, LANES), (per, tok, LANES)
+    w_shape = (per, poles, ROWS, LANES)
+    handed = [
+        jax.ShapeDtypeStruct((1, poles, channels), F32),
+        jax.ShapeDtypeStruct(s_shape, F32),
+        jax.ShapeDtypeStruct(near_shape, F32),
+        jax.ShapeDtypeStruct(w_shape, F32),
+        jax.ShapeDtypeStruct((tok, width), q_feat.dtype),
+        jax.ShapeDtypeStruct((chunks, ROWS, LANES), F32),
+    ]
+    early = []
+    if ahead:
+        handed.append(jax.ShapeDtypeStruct((tok, edge), q_feat.dtype))
+        early = [pltpu.VMEM((tok, edge), q_feat.dtype)]
     args = [
         pltpu.with_memory_space_constraint(x, pltpu.HBM)
         for x in (
             lengths, owners, pole_rate, residue, skip_gain[None, :], k_feat, v_feat, q_feat
         )
     ]
-    return pl.pallas_call(
+    handed = pl.pallas_call(
         functools.partial(kernel, tok=tok, poles=poles, count=count, cols=cols, per=per),
         in_specs=[hbm] * 8,
-        out_specs=[vmem, vmem],
-        out_shape=[
-            jax.ShapeDtypeStruct((tok, channels), q_feat.dtype),
-            jax.ShapeDtypeStruct((1, poles, channels), F32),
-        ],
-        scratch_shapes=[
+        out_specs=[vmem] * len(handed),
+        out_shape=handed,
+        scratch_shapes=early
+        + [pltpu.VMEM(s_shape, F32)] * ahead
+        + [pltpu.VMEM(near_shape, F32)] * ahead
+        + [pltpu.VMEM(w_shape, F32)] * ahead
+        + [
             pltpu.SMEM((count,), jnp.int32), pltpu.SMEM((count,), jnp.int32),
-            feat, feat, feat, state, state, pltpu.VMEM((1, channels), F32), wide, wide,
-            pltpu.VMEM((cols, chunks + 1, poles, LANES), F32),
-            pltpu.VMEM((cols, poles, ROWS, LANES), F32),
+            feat, feat, state, state, pltpu.VMEM((1, channels), F32),
+            pltpu.VMEM((cols, tok, LANES), F32),
             pltpu.VMEM((3, poles, channels), F32),
             pltpu.VMEM((count, poles, channels), F32),
             pltpu.VMEM((3, poles, channels), F32),
@@ -565,9 +639,9 @@
             small, small, small,
             pltpu.VMEM((count + 2, poles, channels), F32),
             state, state, block, block, block, block,
-            pltpu.SMEM((chunks,), jnp.int32), pltpu.SMEM((count,), jnp.int32), pltpu.SMEM((count, ROWS), jnp.int32),
-            pltpu.SMEM((count, ROWS), F32),
-            dma((5,)), dma((tiles, 2)), dma, dma((tiles,)), dma((tiles,)),
+            pltpu.SMEM((chunks,), jnp.int32), pltpu.SMEM((count,), jnp.int32),
+            pltpu.SMEM((count, ROWS), jnp.int32), pltpu.SMEM((count, ROWS), F32),
+            dma((5,)), dma((tiles, 2)), dma((2,)), dma((tiles,)), dma((tiles,)),
             dma((hops, tiles)), dma((hops, tiles)), dma((hops, tiles)), dma((hops, tiles)),
         ],
         compiler_params=pltpu.CompilerParams(
@@ -575,6 +649,18 @@
         ),
         name="modal",
     )(*args)
+    return pl.pallas_call(
+        functools.partial(finish, poles=poles, chunks=chunks, per=per, ahead=ahead),
+        in_specs=[vmem] * len(handed),
+        out_specs=[hbm, hbm],
+        out_shape=[
+            jax.ShapeDtypeStruct((tok, channels), q_feat.dtype),
+            jax.ShapeDtypeStruct((1, poles, channels), F32),
+        ],
+        scratch_shapes=[pltpu.VMEM((tok, width), q_feat.dtype), dma((2 + per,))],
+        compiler_params=pltpu.CompilerParams(vmem_limit_bytes=8 << 20),
+        name="tail",
+    )(*handed)
 
 
 def solution(mesh):

time: 23.1 us -> 22.7 us (0.983)
  local copies, waits for them, and re-layouts: 1.98 us -> 0 us
  Pallas kernels: 20.2 us -> 21.9 us
    pallas_call x0 -> x1, Pallas kernels: none -> 2.05 us  [shards(): pl.pallas_call(functools.partial(finish, poles=poles, chunks=chunks, per=...]
    unnamed x2 -> x0, local copies, waits for them, and re-layouts: 1.98 us -> none
    pallas_call x1, Pallas kernels: 20.2 us -> 19.9 us  [shards(): pl.pallas_call(functools.partial(kernel, tok=tok, poles=poles, count=coun...]
where the time goes in v4:
time: 22.7 us; the launch traced here: 22.6 us
  Pallas kernels  21.9 us (96%)
  between operations  0.64 us (3%)
    pallas_call x1, Pallas kernels, shards(): pl.pallas_call(functools.partial(kernel, tok=tok, poles=poles, count=coun...  19.9 us
    pallas_call x1, Pallas kernels, shards(): pl.pallas_call(functools.partial(finish, poles=poles, chunks=chunks, per=...  2.05 us

profile of v4, /device:TPU:0, one launch (start us, length us, event | category | flops | bytes accessed | tf_op | source)
XLA Modules:
  0.0 22.6 jit_solution(15847293241174384638)
XLA Ops:
  0.6 19.9 %modal.1 = (f32[1,16,2048]{2,1,0:T(8,128)S(1)}, f32[4,65,16,128]{3,2,1,0:T(8,128)S(1)}, f32[4,512,128]{2,1,0:T(8,128)S(1)}, f32[4,16,8,128]{3,2,1,0:T(8,128)S(1)...) custom-call(s32[4]{0:T(128)} %lens_hbm.1, s32[4]{0:T(128)} %own_hbm.1, ...), custom_call_target="tpu_custom_call" | custom-call | tf_op jit(solution)/shard_map/modal/pallas_call | solution.py:622
  20.5 2.1 %tail.1 = (bf16[512,2048]{1,0:T(8,128)(2,1)}, f32[1,16,2048]{2,1,0:T(8,128)}) custom-call(f32[1,16,2048]{2,1,0:T(8,128)S(1)} %get-tuple-element.9.dec_ref, f32[4,65,16,128]{3,2,1,0:T(8,128)S(1)} %get-tuple-element.10.s_ref, f32[4,512,128]{2,1,0:T(8,128)S(1)} %get-tuple-element.11.near_ref, f32[4,16,8,128]{3,2,1,0:T(8,128)S(1)} %get-tuple-element.12.w_ref, ...), custom_call_target="tpu_custom_call" | custom-call | tf_op jit(solution)/shard_map/tail/pallas_call | solution.py:652

commit v5 on v4

--- a/solution.py
+++ b/solution.py
@@ -46,19 +46,20 @@
     lax.fori_loop(0, chunks // EMIT, body, 0)
 
 
-def finish(dec_ref, s_ref, near_ref, w_ref, q_ref, mask_ref, *rest, poles, chunks, per, ahead):
+def finish(dec_ref, s_ref, near_ref, w_ref, q_ref, mask_ref, *rest, poles, chunks, per, late, made):
     rest = list(rest)
-    head_ref = rest.pop(0) if ahead else None
+    head_ref = rest.pop(0) if made else None
     out_hbm, dec_hbm, made_ref, sem = rest
     copies = [pltpu.make_async_copy(dec_ref, dec_hbm, sem.at[0])]
-    edge = ahead * per * LANES
-    if ahead:
+    edge = made * LANES
+    if made:
         copies.append(pltpu.make_async_copy(head_ref, out_hbm.at[:, pl.ds(0, edge)], sem.at[1]))
     for copy in copies:
         copy.start()
-    for c in range(per):
+    for c in range(late):
+        x = per - late + c
         produce(
-            lambda n: mask_ref[n], w_ref.at[c], s_ref.at[c], near_ref.at[c],
+            lambda n: mask_ref[n], w_ref.at[x], s_ref.at[x], near_ref.at[x],
             q_ref, made_ref, lane(c), poles, chunks,
         )
         copies.append(
@@ -75,12 +76,13 @@
 def kernel(
     lens_hbm, own_hbm, rate_hbm, res_hbm, gain_hbm, k_hbm, v_hbm, q_hbm,
     dec_ref, s_out, um_out, w_out, qt_ref, mask_ref, *rest,
-    tok, poles, count, cols, per,
+    tok, poles, count, cols, per, late,
 ):
     tiles = cols // per
     ahead = tiles - 1
     rest = list(rest)
-    out_ref, q_ref = (rest.pop(0), rest.pop(0)) if ahead else (None, None)
+    made = cols - late
+    out_ref, q_ref = (rest.pop(0), rest.pop(0)) if made else (None, None)
     s_all = [rest.pop(0) for _ in range(ahead)] + [s_out]
     um_all = [rest.pop(0) for _ in range(ahead)] + [um_out]
     w_all = [rest.pop(0) for _ in range(ahead)] + [w_out]
@@ -128,9 +130,11 @@
             copy.start()
     params[1].start()
     params[2].start()
-    edge = ahead * width
-    q_loads = [pltpu.make_async_copy(q_hbm.at[:, pl.ds(edge, width)], qt_ref, q_sem.at[0])]
-    if ahead:
+    edge = made * LANES
+    q_loads = [
+        pltpu.make_async_copy(q_hbm.at[:, pl.ds(edge, late * LANES)], qt_ref, q_sem.at[0])
+    ]
+    if made:
         q_loads.append(
             pltpu.make_async_copy(q_hbm.at[:, pl.ds(0, edge)], q_ref, q_sem.at[1])
         )
@@ -383,7 +387,7 @@
             names.append(("carry", g * group // per))
             clock[names[-1]] = now
             now += CARRY_US * per
-        now += EMIT_US * group if g * group < (tiles - 1) * per else 0.0
+        now += EMIT_US * group if g * group < cols - late else 0.0
         names.append(("emit", g))
         clock[names[-1]] = now
     jobs = {name: [] for name in names}
@@ -541,7 +545,7 @@
             def _():
                 carry(t)
 
-        if g * group < ahead * per:
+        if g * group < made:
             each(emit, g)
         serve("emit", g)
 
@@ -593,8 +597,9 @@
     dma = pltpu.SemaphoreType.DMA
     vmem, hbm = pl.BlockSpec(memory_space=pltpu.VMEM), pl.BlockSpec(memory_space=pltpu.HBM)
     ahead = tiles - 1
-    width = per * LANES
-    edge = ahead * width
+    late = max(per // 2, 1)
+    made = cols - late
+    edge = made * LANES
     state = pltpu.VMEM((poles, channels), F32)
     small = pltpu.VMEM((count, ROWS, LANES), F32)
     block = pltpu.VMEM((hops, poles, channels), F32)
@@ -606,11 +611,11 @@
         jax.ShapeDtypeStruct(s_shape, F32),
         jax.ShapeDtypeStruct(near_shape, F32),
         jax.ShapeDtypeStruct(w_shape, F32),
-        jax.ShapeDtypeStruct((tok, width), q_feat.dtype),
+        jax.ShapeDtypeStruct((tok, late * LANES), q_feat.dtype),
         jax.ShapeDtypeStruct((chunks, ROWS, LANES), F32),
     ]
     early = []
-    if ahead:
+    if made:
         handed.append(jax.ShapeDtypeStruct((tok, edge), q_feat.dtype))
         early = [pltpu.VMEM((tok, edge), q_feat.dtype)]
     args = [
@@ -620,7 +625,7 @@
         )
     ]
     handed = pl.pallas_call(
-        functools.partial(kernel, tok=tok, poles=poles, count=count, cols=cols, per=per),
+        functools.partial(kernel, tok=tok, poles=poles, count=count, cols=cols, per=per, late=late),
         in_specs=[hbm] * 8,
         out_specs=[vmem] * len(handed),
         out_shape=handed,
@@ -650,14 +655,14 @@
         name="modal",
     )(*args)
     return pl.pallas_call(
-        functools.partial(finish, poles=poles, chunks=chunks, per=per, ahead=ahead),
+        functools.partial(finish, poles=poles, chunks=chunks, per=per, late=late, made=made),
         in_specs=[vmem] * len(handed),
         out_specs=[hbm, hbm],
         out_shape=[
             jax.ShapeDtypeStruct((tok, channels), q_feat.dtype),
             jax.ShapeDtypeStruct((1, poles, channels), F32),
         ],
-        scratch_shapes=[pltpu.VMEM((tok, width), q_feat.dtype), dma((2 + per,))],
+        scratch_shapes=[pltpu.VMEM((tok, late * LANES), q_feat.dtype), dma((2 + late,))],
         compiler_params=pltpu.CompilerParams(vmem_limit_bytes=8 << 20),
         name="tail",
     )(*handed)

time: 22.7 us -> 22.1 us (0.974)
  Pallas kernels: 21.9 us -> 21.3 us
    pallas_call x1, Pallas kernels: 2.05 us -> 1.38 us  [shards(): pl.pallas_call(functools.partial(finish, poles=poles, chunks=chunks, per=...]
where the time goes in v5:
time: 22.1 us; the launch traced here: 21.9 us
  Pallas kernels  21.3 us (96%)
  between operations  0.64 us (3%)
    pallas_call x1, Pallas kernels, shards(): pl.pallas_call(functools.partial(kernel, tok=tok, poles=poles, count=coun...  19.9 us
    pallas_call x1, Pallas kernels, shards(): pl.pallas_call(functools.partial(finish, poles=poles, chunks=chunks, per=...  1.38 us

profile of v5, /device:TPU:0, one launch (start us, length us, event | category | flops | bytes accessed | tf_op | source)
XLA Modules:
  0.0 21.9 jit_solution(6227316679677882118)
XLA Ops:
  0.6 19.9 %modal.1 = (f32[1,16,2048]{2,1,0:T(8,128)S(1)}, f32[4,65,16,128]{3,2,1,0:T(8,128)S(1)}, f32[4,512,128]{2,1,0:T(8,128)S(1)}, f32[4,16,8,128]{3,2,1,0:T(8,128)S(1)...) custom-call(s32[4]{0:T(128)} %lens_hbm.1, s32[4]{0:T(128)} %own_hbm.1, ...), custom_call_target="tpu_custom_call" | custom-call | tf_op jit(solution)/shard_map/modal/pallas_call | solution.py:627
  20.5 1.4 %tail.1 = (bf16[512,2048]{1,0:T(8,128)(2,1)}, f32[1,16,2048]{2,1,0:T(8,128)}) custom-call(f32[1,16,2048]{2,1,0:T(8,128)S(1)} %get-tuple-element.9.dec_ref, f32[4,65,16,128]{3,2,1,0:T(8,128)S(1)} %get-tuple-element.10.s_ref, f32[4,512,128]{2,1,0:T(8,128)S(1)} %get-tuple-element.11.near_ref, f32[4,16,8,128]{3,2,1,0:T(8,128)S(1)} %get-tuple-element.12.w_ref, ...), custom_call_target="tpu_custom_call" | custom-call | tf_op jit(solution)/shard_map/tail/pallas_call | solution.py:657
